TPU v7x, 32 devices: a whole 2x2x4 slice. The times are simulated.
32 devices in a mesh: seq: 16 (over z, y, x), tp: 2 (over core).
Axes of the slice: x: 2, y: 2, z: 4, core: 2. Of those that a mesh axis runs over, the one named last changes fastest.
Arguments:
- ssm_inputs: bfloat16 [4096, 4096], P('seq', 'tp'), may hold values from -6 to 6
- write_proj: bfloat16 [4096, 128], P('seq'), may hold values from -6 to 6
- read_proj: bfloat16 [4096, 128], P('seq'), may hold values from -0.5 to 0.5
- log_decay: float32 [4096, 64], P('seq', 'tp'), may hold values from -1 to 0, as said below
- skip_gain: float32 [64], P('tp'), may hold values from 0.5 to 1.5
- norm_gain: float32 [4096], replicated, may hold values from 0.1 to 1.9
- gate_weight: bfloat16 [7168, 4096], P('tp', 'seq'), may hold values from -0.09375 to 0.09375
- up_weight: bfloat16 [7168, 4096], P('tp', 'seq'), may hold values from -0.09375 to 0.09375
- down_weight: bfloat16 [7168, 4096], P('tp', 'seq'), may hold values from -0.09375 to 0.09375
Outputs:
- ssd_out: bfloat16 [4096, 4096], P('seq', 'tp')
- mixed: bfloat16 [4096, 4096], P('seq', 'tp')
Inputs may be any that keep to these rules, and one draw needn't show every extreme that they name: `log_decay`: every entry is negative.
All inputs are finite; a program needn't handle non-finite values.
Results may differ from a plain program's by a relative error of at most 0.015.
Values may be sent and summed in bfloat16 or wider, within the bound.
A program may use at most 192 MiB of HBM per device.

v0:
```python
import jax
import jax.numpy as jnp
from jax import lax
from jax.sharding import PartitionSpec as P

BLOCK = 128


HIGHEST = lax.Precision.HIGHEST


def shifted(block, axis, distance):
    devices = range(lax.axis_size(axis))
    route = [(i - distance, i) for i in devices if i - distance in devices]
    return lax.ppermute(block, axis, route)


def block_step(carried_state, pieces):
    feature_rows, write_rows, read_rows, decay_rows = pieces
    scaled = feature_rows * jnp.sqrt(-jnp.expm1(2.0 * decay_rows))[:, :, None]
    running = jnp.cumsum(decay_rows, axis=0)
    span_len = decay_rows.shape[0]
    causal = jnp.arange(span_len)[:, None] >= jnp.arange(span_len)[None, :]
    spread_log = running[:, None, :] - running[None, :, :]
    weights = jnp.exp(jnp.where(causal[:, :, None], spread_log, -jnp.inf))
    scores = jnp.dot(read_rows, write_rows.T, precision=HIGHEST)
    within = jnp.einsum("ijh,jhp->ihp", scores[:, :, None] * weights, scaled, precision=HIGHEST)
    arriving = jnp.exp(running)[:, :, None] * jnp.einsum(
        "hpn,in->ihp", carried_state, read_rows, precision=HIGHEST
    )
    to_end = jnp.exp(running[-1][None, :] - running)
    written = jnp.einsum("jhp,jn->hpn", scaled * to_end[:, :, None], write_rows, precision=HIGHEST)
    next_state = jnp.exp(running[-1])[:, None, None] * carried_state + written
    return (next_state, within + arriving)


def hand_over(outgoing):
    return shifted(outgoing.astype(jnp.bfloat16), "seq", 1).astype(outgoing.dtype)


def on_device(
    ssm_inputs,
    write_proj,
    read_proj,
    log_decay,
    skip_gain,
    norm_gain,
    gate_weight,
    up_weight,
    down_weight,
):
    tok_rows, feature_count = ssm_inputs.shape
    head_count = log_decay.shape[1]
    head_width = feature_count // head_count
    state_width = write_proj.shape[1]
    block_count = tok_rows // BLOCK
    features = ssm_inputs.astype(jnp.float32).reshape(tok_rows, head_count, head_width)
    writes = write_proj.astype(jnp.float32)
    reads = read_proj.astype(jnp.float32)
    start_state = jnp.zeros((head_count, head_width, state_width), jnp.float32)
    pieces = (
        features.reshape(block_count, BLOCK, head_count, head_width),
        writes.reshape(block_count, BLOCK, state_width),
        reads.reshape(block_count, BLOCK, state_width),
        log_decay.reshape(block_count, BLOCK, head_count),
    )
    local_final, outputs = lax.scan(block_step, start_state, pieces)
    running = jnp.cumsum(log_decay, axis=0)
    whole_decay = jnp.exp(running[-1])

    def one_turn(turn, outgoing):
        return whole_decay[:, None, None] * hand_over(outgoing) + local_final

    outgoing = lax.fori_loop(0, lax.axis_size("seq") - 1, one_turn, local_final)
    incoming = hand_over(outgoing)
    arriving = jnp.exp(running)[:, :, None] * jnp.einsum(
        "hpn,in->ihp", incoming, reads, precision=HIGHEST
    )
    combined = (
        outputs.reshape(tok_rows, head_count, head_width)
        + arriving
        + skip_gain[None, :, None] * features
    )
    ssd_out = combined.reshape(tok_rows, feature_count).astype(jnp.bfloat16)
    gathered = lax.all_gather(ssd_out, "tp", axis=1, tiled=True)
    rows_f = gathered.astype(jnp.float32)
    mean_sq = jnp.mean(rows_f * rows_f, axis=1, keepdims=True)
    normed = (rows_f * lax.rsqrt(mean_sq + 1e-05) * norm_gain[None, :]).astype(jnp.bfloat16)
    gate_part = lax.dot_general(
        normed,
        lax.all_gather(gate_weight, "seq", axis=1, tiled=True),
        (((1,), (1,)), ((), ())),
        preferred_element_type=jnp.float32,
    )
    up_part = lax.dot_general(
        normed,
        lax.all_gather(up_weight, "seq", axis=1, tiled=True),
        (((1,), (1,)), ((), ())),
        preferred_element_type=jnp.float32,
    )
    hidden = (jax.nn.silu(gate_part) * up_part).astype(jnp.bfloat16)
    partial_value = jnp.dot(
        hidden,
        lax.all_gather(down_weight, "seq", axis=1, tiled=True),
        preferred_element_type=jnp.float32,
    )
    own_part = lax.psum_scatter(
        partial_value.astype(jnp.bfloat16), "tp", scatter_dimension=1, tiled=True
    ).astype(jnp.float32)
    mixed = (ssd_out.astype(jnp.float32) + own_part).astype(jnp.bfloat16)
    return (ssd_out, mixed)


def solution(mesh):
    placed = (
        P("seq", "tp"),
        P("seq", None),
        P("seq", None),
        P("seq", "tp"),
        P("tp"),
        P(),
        P("tp", "seq"),
        P("tp", "seq"),
        P("tp", "seq"),
    )
    return jax.shard_map(
        on_device,
        mesh=mesh,
        in_specs=placed,
        out_specs=(P("seq", "tp"), P("seq", "tp")),
        check_vma=False,
    )
```

profile of v0, /device:TPU:0, one launch (start us, length us, event | category | flops | bytes accessed | tf_op | source)
XLA Modules:
  0.0 2215.5 jit_solution(16742776819202182858)
XLA Ops:
  7.2 1.4 reshape.99
  8.6 1.4 copy_bitcast_fusion
  10.0 4.5 reshape.115
  14.5 4.8 copy.74
  19.3 72.8 %while.24 = (s32[]{:T(128)}, f32[32,64,128]{2,1,0:T(8,128)S(1)}, f32[2,128,32,64]{1,0,3,2:T(2,128)}, f32[2,128,32]{1,0,2:T(2,128)}, f32[2,128,32,64]{1,3,2,0:T(8...) while((s32[]{:T(128)}, f32[32,64,128]{2,1,0:T(8,128)S(1)}, ...), condition=%wide.region_2.3_spmd.clone, body=%wide.region_0.2_spmd.clone.sunk | while | flops 1237606400 | bytes 11292416 | solution.py:67
  20.5 1.0 convolution_multiply_fusion.3
  22.5 5.5 fusion.99
  28.0 24.9 %dynamic_update_slice.6 = f32[2,128,32,64]{1,0,3,2:T(2,128)} dynamic-update-slice(f32[2,128,32,64]{1,0,3,2:T(2,128)} %get-tuple-element.235, f32[1,128,32,64]{1,0,3,2:T(1,128)S(1)} %bitcast.102, s32[]{:T(128)} %get-tuple-element.233, s32[]{:T(128)} %constant.38.clone.1..sunk, s32[]{:T(128)} %constant.38.clone.1..sunk, s32[]{:T(128)} %constant.38.clone.1..sunk) | dynamic-update-slice | bytes 2097156 | tf_op jit(solution)/shard_map/while/body/jit(dynamic_update_index_in_dim)/dynamic_update_slice | solution.py:67
  52.9 2.8 convolution_add_fusion.2
  56.9 1.0 convolution_multiply_fusion.3
  58.9 5.5 fusion.99
  64.4 24.9 %dynamic_update_slice.6 = f32[2,128,32,64]{1,0,3,2:T(2,128)} dynamic-update-slice(f32[2,128,32,64]{1,0,3,2:T(2,128)} %get-tuple-element.235, f32[1,128,32,64]{1,0,3,2:T(1,128)S(1)} %bitcast.102, s32[]{:T(128)} %get-tuple-element.233, s32[]{:T(128)} %constant.38.clone.1..sunk, s32[]{:T(128)} %constant.38.clone.1..sunk, s32[]{:T(128)} %constant.38.clone.1..sunk) | dynamic-update-slice | bytes 2097156 | tf_op jit(solution)/shard_map/while/body/jit(dynamic_update_index_in_dim)/dynamic_update_slice | solution.py:67
  89.3 2.8 convolution_add_fusion.2
  93.0 1.3 reduce-window.6
  94.8 242.6 %while.23 = (s32[]{:T(128)}, bf16[32,64,128]{2,1,0:T(8,128)(2,1)}, f32[32]{0:T(128)S(1)}, f32[32,64,128]{2,1,0:T(8,128)S(1)}, s32[]{:T(128)}) while((s32[]{:T(128)}, bf16[32,64,128]{2,1,0:T(8,128)(2,1)}, f32[32]{0:T(128)S(1)}, f32[32,64,128]{2,1,0:T(8,128)S(1)}, s32[]{:T(128)}) %tuple.54), condition=%wide.region_6.7_spmd, body=%wide.region_5.6_spmd.sunk | while | flops 1048578 | bytes 4194533 | solution.py:74
  94.8 4.9 collective-permute-start
  99.6 11.4 collective-permute-done
  111.1 1.0 multiply_add_fusion.2
  112.1 4.3 collective-permute-start
  116.4 10.6 collective-permute-done
  127.0 1.0 multiply_add_fusion.2
  128.0 4.3 collective-permute-start
  132.3 9.7 collective-permute-done
  142.0 1.0 multiply_add_fusion.2
  143.0 5.2 collective-permute-start
  148.2 8.7 collective-permute-done
  157.9 5.2 collective-permute-start
  163.1 7.8 collective-permute-done
  171.9 5.2 collective-permute-start
  177.1 7.0 collective-permute-done
  185.1 5.2 collective-permute-start
  190.3 7.0 collective-permute-done
  198.3 5.2 collective-permute-start
  203.5 7.0 collective-permute-done
  211.5 6.1 collective-permute-start
  217.6 7.8 collective-permute-done
  226.4 6.7 collective-permute-start
  233.1 8.9 collective-permute-done
  242.9 7.0 collective-permute-start
  249.9 9.9 collective-permute-done
  260.9 7.0 collective-permute-start
  267.8 11.0 collective-permute-done
  279.9 7.0 collective-permute-start
  286.9 12.3 collective-permute-done
  300.2 7.0 collective-permute-start
  307.2 11.8 collective-permute-done
  320.0 5.8 collective-permute-start
  325.8 10.6 collective-permute-done
  337.3 5.3 collective-permute-start.1
  342.6 1.5 copy.78
  344.1 4.0 reshape.104
  348.2 1.4 collective-permute-done.1
  349.6 3.0 fusion.54
  354.9 18.5 all-gather.5.cloned.1.call-done
  373.5 2.3 fusion.44
  375.8 600.1 %all-gather.7.cloned.1.call-done = bf16[3584,4096]{1,0:T(8,128)(2,1)} async-done(((bf16[3584,256]{1,0:T(8,128)(2,1)}), bf16[3584,4096]{1,0:T(8,128)(2,1)}) %all-gather.7.cloned.1.call-update) | async-done | bytes 29360144 | tf_op jit(solution)/shard_map/all_gather | solution.py:91
  975.9 15.4 fusion.58
  991.3 587.0 %all-gather.9.cloned.1.call-done = bf16[3584,4096]{1,0:T(8,128)(2,1)} async-done(((bf16[3584,256]{1,0:T(8,128)(2,1)}), bf16[3584,4096]{1,0:T(8,128)(2,1)}) %all-gather.9.cloned.1.call-update) | async-done | bytes 29360144 | tf_op jit(solution)/shard_map/all_gather | solution.py:97
  1578.3 16.9 fusion.43.clone.4
  1595.2 585.4 %all-gather.11.cloned.1.call-done = bf16[3584,4096]{1,0:T(8,128)(2,1)} async-done(((bf16[3584,256]{1,0:T(8,128)(2,1)}), bf16[3584,4096]{1,0:T(8,128)(2,1)}) %all-gather.11.cloned.1.call-update) | async-done | bytes 29360144 | tf_op jit(solution)/shard_map/all_gather | solution.py:104
  2180.6 14.8 convolution_convert_fusion
  2195.4 1.2 copy-done
  2197.3 9.1 reduce-scatter.2.cloned.1.call-done
  2206.4 2.6 add_convert_fusion
  (74 shorter events, 20.8 us)
Async XLA Ops:
  7.2 366.3 %all-gather.5.cloned.1.call-start = ((), (), s32[]{:S(2)}) async-start(), calls=%async_computation.1 | async-start | bytes 3145728 | tf_op jit(solution)/shard_map/all_gather | solution.py:85
  14.5 4.8 copy-start.5
  14.5 4.8 copy-start.3
  94.8 16.3 collective-permute-start
  112.1 14.9 collective-permute-start
  128.0 14.0 collective-permute-start
  143.0 13.9 collective-permute-start
  157.9 13.0 collective-permute-start
  171.9 12.2 collective-permute-start
  185.1 12.2 collective-permute-start
  198.3 12.2 collective-permute-start
  211.5 13.9 collective-permute-start
  226.4 15.6 collective-permute-start
  242.9 16.9 collective-permute-start
  260.9 18.0 collective-permute-start
  279.9 19.3 collective-permute-start
  300.2 18.8 collective-permute-start
  320.0 16.4 collective-permute-start
  337.3 12.2 collective-permute-start.1
  344.1 5.5 copy-start.4
  344.1 5.5 copy-start.6
  352.6 623.2 %all-gather.7.cloned.1.call-start = ((), (), s32[]{:S(2)}) async-start(), calls=%async_computation.2 | async-start | bytes 31195136 | tf_op jit(solution)/shard_map/all_gather | solution.py:91
  353.4 1224.9 %all-gather.9.cloned.1.call-start = ((), (), s32[]{:S(2)}) async-start(), calls=%async_computation.3 | async-start | bytes 31195136 | tf_op jit(solution)/shard_map/all_gather | solution.py:97
  354.1 621.7 %copy-start.7 = (f32[4096]{0:T(1024)S(1)}, f32[4096]{0:T(1024)}, u32[]{:S(2)}) copy-start(f32[4096]{0:T(1024)} %param.18) | copy-start | bytes 49156
  354.1 1826.5 %all-gather.11.cloned.1.call-start = ((), (), s32[]{:S(2)}) async-start(), calls=%async_computation.4 | async-start | bytes 31195136 | tf_op jit(solution)/shard_map/all_gather | solution.py:104
  354.7 1851.7 %reduce-scatter.2.cloned.1.call-start = ((), (), s32[]{:S(2)}) async-start(), calls=%async_computation.5 | async-start | bytes 3145728 | tf_op jit(solution)/shard_map/reduce_scatter | solution.py:107
  373.5 602.4 %copy-start.2 = (bf16[256,4096]{0,1:T(8,128)(2,1)S(1)}, bf16[256,4096]{0,1:T(8,128)(2,1)}, u32[]{:S(2)}) copy-start(bf16[256,4096]{0,1:T(8,128)(2,1)} %all-gather.5.cloned.1.call-done) | copy-start | bytes 6291460
  2195.4 1.2 copy-start
  2197.3 11.7 copy-start.1
Sparse Core Ops, SparseCore 0:
  352.7 20.6 all-gather.4
  374.9 600.8 all-gather.6
  977.3 600.9 all-gather.8
  1579.6 600.9 all-gather.10
  2195.6 10.8 reduce-scatter.1
where the time goes:
time: 2220 us
  waiting for transfers between devices  1940 us (87%)
  starting transfers between devices  91.8 us (4%)
  local copies, waits for them, and re-layouts  72.8 us (3%)
  matrix products  69.2 us (3%)
  other arithmetic  22.7 us (1%)
    all_gather x1, waiting for transfers between devices, on_device(): lax.all_gather(gate_weight, 'seq', axis=1, tiled=True)  600 us
    all_gather x1, waiting for transfers between devices, on_device(): lax.all_gather(up_weight, 'seq', axis=1, tiled=True)  587 us
    all_gather x1, waiting for transfers between devices, on_device(): lax.all_gather(down_weight, 'seq', axis=1, tiled=True)  585 us
    ppermute x16, waiting for transfers between devices, shifted(): return lax.ppermute(block, axis, route)  143 us
    ppermute x16, starting transfers between devices, shifted(): return lax.ppermute(block, axis, route)  91.4 us
    dynamic_update_slice x2, local copies, waits for them, and re-layouts, on_device(): local_final, outputs = lax.scan(block_step, start_state, pieces)  49.7 us
  transfers between devices with their start and end apart: 21, of which 21 were waited for; matrix products, arithmetic and copies ran while one was open for 2% of the time, Pallas kernels for 0%

commit v1 on v0

v1 whole, which is shorter than its diff:
```python
import functools

import jax
import jax.numpy as jnp
from jax import lax
from jax.experimental import pallas as pl
from jax.experimental.pallas import tpu as pltpu
from jax.sharding import PartitionSpec as P

MINOR = 4
BF = jnp.bfloat16
F32 = jnp.float32


def flip(b, m):
    if m == 0:
        return b
    if m == 1:
        return b + 1 - 2 * (b % 2)
    if m == 2:
        return (b + 2) % 4
    return 3 - b


def along_major(x, step, n):
    major = n // MINOR
    route = [
        (a * MINOR + b, ((a + step) % major) * MINOR + b)
        for a in range(major)
        for b in range(MINOR)
    ]
    return lax.ppermute(x, "seq", route)


def along_minor(x, m, n):
    route = [(i, (i // MINOR) * MINOR + flip(i % MINOR, m)) for i in range(n)]
    return lax.ppermute(x, "seq", route)


def nt(x, w):
    return lax.dot_general(x, w, (((1,), (1,)), ((), ())), preferred_element_type=F32)


def piece_ref(refs, k, m):
    group, at = refs[5 * (k // 2) : 5 * (k // 2) + 5], k % 2
    if m < 3:
        return group[m].at[at]
    return group[3 + at].at[0]


def gate_up_kernel(major, depth, *args):
    count = 5 * major // 2
    x_ref, w_refs = args[0], args[1 : 1 + count]
    h_ref, wbuf, acc, sem = args[1 + count :]
    rows = x_ref.shape[0]
    tile = min(rows, 256)
    me = lax.axis_index("seq")
    a, b = me // MINOR, me % MINOR

    def fetch(k):
        return [
            pltpu.make_async_copy(
                piece_ref(w_refs, k, m).at[pl.ds(0, 2)], wbuf.at[k % 2, m], sem.at[k % 2, m]
            )
            for m in range(MINOR)
        ]

    for c in fetch(0):
        c.start()
    for k in range(major):
        if k + 1 < major:
            for c in fetch(k + 1):
                c.start()
        for c in fetch(k):
            c.wait()
        src = (a + major - k) % major
        cols = [
            pl.ds(pl.multiple_of((src * MINOR + flip(b, m)) * depth, depth), depth)
            for m in range(MINOR)
        ]

        @pl.loop(0, rows // tile)
        def _(i):
            at = pl.ds(pl.multiple_of(i * tile, tile), tile)
            sums = [None, None]
            for m in range(MINOR):
                x = x_ref[at, cols[m]]
                for q in range(2):
                    d = nt(x, wbuf[k % 2, m, q])
                    sums[q] = d if sums[q] is None else sums[q] + d
            if k > 0:
                sums = [acc[q, at, :] + sums[q] for q in range(2)]
            if k + 1 < major:
                for q in range(2):
                    acc[q, at, :] = sums[q]
            else:
                g, u = sums
                h_ref[at, :] = (g / (1.0 + jnp.exp(-g)) * u).astype(BF)


def down_kernel(major, depth, *args):
    count = 5 * major // 2
    h_ref, w_refs = args[0], args[1 : 1 + count]
    o_ref, wbuf, obuf, sem, osem = args[1 + count :]
    rows = h_ref.shape[0]
    tile = min(rows, 256)
    me = lax.axis_index("seq")
    a, b = me // MINOR, me % MINOR
    steps = [(k, m) for k in range(major) for m in range(MINOR)]

    def fetch(j):
        k, m = steps[j]
        return pltpu.make_async_copy(piece_ref(w_refs, k, m).at[2], wbuf.at[j % 2], sem.at[j % 2])

    def put(j):
        k, m = steps[j]
        src = (a + major - k) % major
        col = pl.multiple_of((src * MINOR + flip(b, m)) * depth, depth)
        return pltpu.make_async_copy(obuf.at[j % 2], o_ref.at[:, pl.ds(col, depth)], osem.at[j % 2])

    fetch(0).start()
    for j in range(len(steps)):
        if j + 1 < len(steps):
            fetch(j + 1).start()
        fetch(j).wait()
        if j >= 2:
            put(j - 2).wait()

        @pl.loop(0, rows // tile)
        def _(i):
            at = pl.ds(pl.multiple_of(i * tile, tile), tile)
            obuf[j % 2, at, :] = jnp.dot(
                h_ref[at, :], wbuf[j % 2], preferred_element_type=F32
            ).astype(BF)

        put(j).start()
    put(len(steps) - 2).wait()
    put(len(steps) - 1).wait()


ANY = pl.BlockSpec(memory_space=pl.ANY)
INV = pl.BlockSpec(memory_space=pltpu.VMEM)


def feed_forward(normed, pieces, major, depth):
    rows, width = normed.shape
    units = pieces[0].shape[2]
    hidden = pl.pallas_call(
        functools.partial(gate_up_kernel, major, depth),
        out_shape=jax.ShapeDtypeStruct((rows, units), BF),
        in_specs=[INV] + [ANY] * len(pieces),
        out_specs=INV,
        scratch_shapes=[
            pltpu.VMEM((2, MINOR, 2, units, depth), BF),
            pltpu.VMEM((2, rows, units), F32),
            pltpu.SemaphoreType.DMA((2, MINOR)),
        ],
        compiler_params=pltpu.CompilerParams(vmem_limit_bytes=56 << 20),
        cost_estimate=pl.CostEstimate(
            flops=4 * rows * units * width, bytes_accessed=4 * units * width, transcendentals=0
        ),
    )(normed, *pieces)
    return pl.pallas_call(
        functools.partial(down_kernel, major, depth),
        out_shape=jax.ShapeDtypeStruct((rows, width), BF),
        in_specs=[INV] + [ANY] * len(pieces),
        out_specs=ANY,
        scratch_shapes=[
            pltpu.VMEM((2, units, depth), BF),
            pltpu.VMEM((2, rows, depth), BF),
            pltpu.SemaphoreType.DMA((2,)),
            pltpu.SemaphoreType.DMA((2,)),
        ],
        compiler_params=pltpu.CompilerParams(vmem_limit_bytes=40 << 20),
        cost_estimate=pl.CostEstimate(
            flops=2 * rows * units * width, bytes_accessed=4 * units * width, transcendentals=0
        ),
    )(hidden, *pieces)


def on_device(
    ssm_inputs,
    write_proj,
    read_proj,
    log_decay,
    skip_gain,
    norm_gain,
    gate_weight,
    up_weight,
    down_weight,
):
    n = lax.axis_size("seq")
    tp = lax.axis_size("tp")
    major = n // MINOR
    me = lax.axis_index("seq")
    a = me // MINOR
    toks, feats = ssm_inputs.shape
    heads = log_decay.shape[1]
    hdim = feats // heads
    states = write_proj.shape[1]
    units, depth = gate_weight.shape
    part = units // major

    stacked = jnp.stack([w.reshape(major, part, depth) for w in (gate_weight, up_weight, down_weight)])

    def chunk(k):
        return lax.dynamic_index_in_dim(stacked, (a + k) % major, axis=1, keepdims=False)

    got = [chunk(0)] + [along_major(chunk(k), k, n) for k in range(1, major)]
    pieces = []
    for g in range(0, major, 2):
        own = jnp.stack(got[g : g + 2])
        over_x = along_minor(own, 1, n)
        over_y = along_minor(own, 2, n)
        first = along_minor(over_x[:1], 2, n)
        second = along_minor(over_y[1:], 1, n)
        pieces += [own, over_x, over_y, first, second]

    x = ssm_inputs.astype(F32).reshape(toks, heads, hdim)
    scaled = x * jnp.sqrt(-jnp.expm1(2.0 * log_decay))[:, :, None]
    running = jnp.cumsum(log_decay, axis=0)
    total = running[-1]
    to_end = jnp.exp(total[None, :] - running)
    local_final = lax.dot_general(
        (scaled * to_end[:, :, None]).astype(BF).reshape(toks, feats),
        write_proj,
        (((0,), (0,)), ((), ())),
        preferred_element_type=F32,
    )
    rows = feats // n
    row_total = jnp.repeat(total, hdim).reshape(n, rows)
    finals = lax.all_to_all(
        local_final.astype(BF).reshape(n, rows, states), "seq", 0, 0, tiled=True
    ).astype(F32)
    decays = jnp.exp(lax.all_to_all(row_total, "seq", 0, 0, tiled=True))
    state = jnp.zeros((rows, states), F32)
    before = []
    for j in range(n):
        before.append(state.astype(BF))
        if j + 1 < n:
            state = decays[j][:, None] * state + finals[j]
    incoming = lax.all_to_all(jnp.stack(before), "seq", 0, 0, tiled=True).reshape(feats, states)

    scores = nt(read_proj, write_proj)
    r = running.T
    causal = jnp.arange(toks)[:, None] >= jnp.arange(toks)[None, :]
    weights = jnp.exp(jnp.where(causal[None], r[:, :, None] - r[:, None, :], -jnp.inf))
    mixing = (scores[None] * weights).astype(BF)
    within = jnp.einsum(
        "hij,hjp->hip", mixing, scaled.astype(BF).transpose(1, 0, 2), preferred_element_type=F32
    ).transpose(1, 0, 2)
    arriving = nt(read_proj, incoming).reshape(toks, heads, hdim)
    combined = within + jnp.exp(running)[:, :, None] * arriving + skip_gain[None, :, None] * x
    ssd_out = combined.reshape(toks, feats).astype(BF)

    rows_f = ssd_out.astype(F32)
    square_sum = lax.psum(jnp.sum(rows_f * rows_f, axis=1, keepdims=True), "tp")
    gain = lax.dynamic_slice_in_dim(norm_gain, lax.axis_index("tp") * feats, feats)
    normed = (rows_f * lax.rsqrt(square_sum / (feats * tp) + 1e-05) * gain[None, :]).astype(BF)

    group = jnp.concatenate([normed] + [along_major(normed, k, n) for k in range(1, major)], axis=0)
    group = lax.all_gather(group, "tp", axis=1, tiled=True)
    partial = feed_forward(group, pieces, major, depth)
    own = lax.psum_scatter(partial, "tp", scatter_dimension=1, tiled=True)
    own = own.reshape(major, toks, feats)
    mlp = own[0].astype(F32)
    for k in range(1, major):
        mlp = mlp + along_major(own[k], major - k, n).astype(F32)
    mixed = (rows_f + mlp).astype(BF)
    return (ssd_out, mixed)


def solution(mesh):
    placed = (
        P("seq", "tp"),
        P("seq", None),
        P("seq", None),
        P("seq", "tp"),
        P("tp"),
        P(),
        P("tp", "seq"),
        P("tp", "seq"),
        P("tp", "seq"),
    )
    return jax.shard_map(
        on_device,
        mesh=mesh,
        in_specs=placed,
        out_specs=(P("seq", "tp"), P("seq", "tp")),
        check_vma=False,
    )
```

time: 2220 us -> 610 us (0.27)
  waiting for transfers between devices: 1940 us -> 458 us
  matrix products: 69.2 us -> 4.82 us
  local copies, waits for them, and re-layouts: 72.8 us -> 11.2 us
  starting transfers between devices: 91.8 us -> 34.8 us
  Pallas kernels: 0 us -> 49.4 us
    all_gather x4 -> x1, waiting for transfers between devices: 1790 us -> 0.01 us  [on_device(): group = lax.all_gather(group, 'tp', axis=1, tiled=True)]
    ppermute x16 -> x17, waiting for transfers between devices: 143 us -> 379 us  [the longest x9 266 us: along_major(): return lax.ppermute(x, 'seq', route)]
    ppermute x16 -> x17, starting transfers between devices: 91.4 us -> 18.7 us  [the longest x9 11.6 us: along_major(): return lax.ppermute(x, 'seq', route)]
    dot_general x12 -> x4, matrix products: 69.2 us -> 4.82 us  [the longest x1 2.98 us: on_device(): jnp.einsum('hij,hjp->hip', mixing, scaled.astype(BF).transpose(1, 0, 2),...]
    dynamic_update_slice x2 -> x0, local copies, waits for them, and re-layouts: 49.7 us -> none  [on_device(): local_final, outputs = lax.scan(block_step, start_state, pieces)]
    pallas_call x0 -> x2, Pallas kernels: none -> 49.4 us  [the longest x1 27.9 us: feed_forward(): pl.pallas_call(functools.partial(gate_up_kernel, major, depth), out_shape...]
    reduce_scatter x1, waiting for transfers between devices: 9.12 us -> 47.4 us  [on_device(): own = lax.psum_scatter(partial, 'tp', scatter_dimension=1, tiled=True)]
    all_to_all x0 -> x3, waiting for transfers between devices: none -> 31.3 us  [the longest x1 14.1 us: on_device(): lax.all_to_all(jnp.stack(before), 'seq', 0, 0, tiled=True)]
  transfers between devices with their start and end apart: 21 -> 22, of which waited for: 21 -> 15; matrix products, arithmetic and copies ran while one was open for 2% -> 1% of each run, Pallas kernels for 0% -> 0%
where the time goes in v1:
time: 610 us; the launch traced here: 608 us
  waiting for transfers between devices  458 us (75%)
  Pallas kernels  49.4 us (8%)
  starting transfers between devices  34.8 us (6%)
  other arithmetic  33.2 us (5%)
  between operations  14.5 us (2%)
  local copies, waits for them, and re-layouts  11.2 us (2%)
    ppermute x9, waiting for transfers between devices, along_major(): return lax.ppermute(x, 'seq', route)  266 us
    ppermute x8, waiting for transfers between devices, along_minor(): return lax.ppermute(x, 'seq', route)  113 us
    reduce_scatter x1, waiting for transfers between devices, on_device(): own = lax.psum_scatter(partial, 'tp', scatter_dimension=1, tiled=True)  47.4 us
    pallas_call x1, Pallas kernels, feed_forward(): pl.pallas_call(functools.partial(gate_up_kernel, major, depth), out_shape...  27.9 us
    pallas_call x1, Pallas kernels, feed_forward(): pl.pallas_call(functools.partial(down_kernel, major, depth), out_shape=ja...  21.5 us
    unnamed x14, other arithmetic  20.3 us
    all_to_all x1, waiting for transfers between devices, on_device(): lax.all_to_all(jnp.stack(before), 'seq', 0, 0, tiled=True)  14.1 us
    all_to_all x1, waiting for transfers between devices, on_device(): lax.all_to_all(local_final.astype(BF).reshape(n, rows, states), 'seq', 0,...  13.9 us
  transfers between devices with their start and end apart: 22, of which 15 were waited for; matrix products, arithmetic and copies ran while one was open for 1% of the time, Pallas kernels for 0%

profile of v1, /device:TPU:0, one launch (start us, length us, event | category | flops | bytes accessed | tf_op | source)
XLA Modules:
  0.0 608.5 jit_solution(16577306492061827962)
XLA Ops:
  7.2 0.8 copy_bitcast_fusion.1
  8.0 0.6 reduce-window.6
  9.2 0.7 all_to_all.12
  9.9 8.3 %all-to-all-start = ((f32[16,1,128]{2,1,0:T(1,128)}), f32[16,1,128]{2,1,0:T(1,128)S(1)}, u32[]{:S(2)}, u32[]{:S(2)}) async-start(f32[16,1,128]{2,1,0:T(1,128)} %all_to_all.12), calls=%async_computation | async-start | bytes 16384 | tf_op jit(solution)/shard_map/all_to_all | solution.py:235
  18.2 0.8 bitcast_exponential_fusion
  19.1 1.5 copy.31
  20.9 1.2 convolution_convert_fusion
  22.1 3.3 all-to-all-done
  25.4 3.6 all-to-all-start.1
  29.0 0.6 constant_dynamic-update-slice_fusion.15
  29.7 13.9 %all-to-all-done.1 = bf16[16,128,128]{2,1,0:T(8,128)(2,1)S(1)} async-done(((bf16[16,128,128]{2,1,0:T(8,128)(2,1)}), bf16[16,128,128]{2,1,0:T(8,128)(2,1)S(1)}, u32[]{:S(2)}, u32[]{:S(2)}) %all-to-all-start.1) | async-done | bytes 524320 | tf_op jit(solution)/shard_map/all_to_all | solution.py:232
  43.7 0.8 constant_dynamic-update-slice_fusion.14
  44.5 0.7 constant_dynamic-update-slice_fusion.13
  45.3 1.5 constant_dynamic-update-slice_fusion.12
  46.8 1.6 constant_dynamic-update-slice_fusion.11
  48.4 1.5 constant_dynamic-update-slice_fusion.10
  49.9 1.6 constant_dynamic-update-slice_fusion.9
  51.5 1.5 constant_dynamic-update-slice_fusion.8
  53.1 1.6 constant_dynamic-update-slice_fusion.7
  54.7 1.5 constant_dynamic-update-slice_fusion.6
  56.2 1.6 constant_dynamic-update-slice_fusion.5
  57.8 1.5 constant_dynamic-update-slice_fusion.4
  59.3 1.6 constant_dynamic-update-slice_fusion.3
  60.9 1.5 constant_dynamic-update-slice_fusion.2
  62.5 1.6 constant_dynamic-update-slice_fusion.1
  64.1 1.5 constant_dynamic-update-slice_fusion
  65.6 4.0 all-to-all-start.2
  69.9 14.1 %all-to-all-done.2 = bf16[16,128,128]{2,1,0:T(8,128)(2,1)S(1)} async-done(((bf16[16,128,128]{2,1,0:T(8,128)(2,1)}), bf16[16,128,128]{2,1,0:T(8,128)(2,1)S(1)}, u32[]{:S(2)}, u32[]{:S(2)}) %all-to-all-start.2) | async-done | bytes 524320 | tf_op jit(solution)/shard_map/all_to_all | solution.py:242
  84.5 3.0 multiply_reduce_fusion
  87.5 2.5 psum.7
  90.0 0.6 copy.36
  90.9 1.9 collective-permute-start.2
  92.8 0.9 collective-permute-start.1
  93.7 22.7 %collective-permute-done.2 = bf16[256,2048]{1,0:T(8,128)(2,1)S(1)} collective-permute-done((bf16[256,2048]{1,0:T(8,128)(2,1)S(1)}, bf16[256,2048]{1,0:T(8,128)(2,1)S(1)}, u32[]{:S(2)}, u32[]{:S(2)}) %collective-permute-start.2) | collective-permute-done | bytes 1048608 | tf_op jit(solution)/shard_map/ppermute | solution.py:32
  116.4 67.9 %collective-permute-done.1 = bf16[256,2048]{1,0:T(8,128)(2,1)S(1)} collective-permute-done((bf16[256,2048]{1,0:T(8,128)(2,1)S(1)}, bf16[256,2048]{1,0:T(8,128)(2,1)S(1)}, u32[]{:S(2)}, u32[]{:S(2)}) %collective-permute-start.1) | collective-permute-done | bytes 1048608 | tf_op jit(solution)/shard_map/ppermute | solution.py:32
  184.3 2.3 pad_maximum_fusion.1
  186.8 1.3 copy-done.14
  188.1 3.2 pad_maximum_fusion
  191.8 1.1 collective-permute-start.8
  192.9 2.8 collective-permute-start.9
  195.7 31.0 %collective-permute-done.3 = bf16[3,896,256]{2,1,0:T(8,128)(2,1)S(1)} collective-permute-done((bf16[3,896,256]{2,1,0:T(8,128)(2,1)S(1)}, bf16[3,896,256]{2,1,0:T(8,128)(2,1)S(1)}, u32[]{:S(2)}, u32[]{:S(2)}) %collective-permute-start.3) | collective-permute-done | bytes 1376288 | tf_op jit(solution)/shard_map/ppermute | solution.py:32
  227.0 0.8 collective-permute-start.5
  227.8 0.6 collective-permute-start.4
  228.4 55.6 %collective-permute-done.8 = bf16[3,896,256]{2,1,0:T(8,128)(2,1)S(1)} collective-permute-done((bf16[3,896,256]{2,1,0:T(8,128)(2,1)S(1)}, bf16[3,896,256]{2,1,0:T(8,128)(2,1)S(1)}, u32[]{:S(2)}, u32[]{:S(2)}) %collective-permute-start.8) | collective-permute-done | bytes 1376288 | tf_op jit(solution)/shard_map/ppermute | solution.py:32
  284.3 1.0 collective-permute-start.11
  285.2 0.6 collective-permute-start.10
  285.9 1.5 collective-permute-start.7
  287.6 1.2 collective-permute-start.6
  288.7 58.2 %collective-permute-done.11.args_8_ = bf16[2,3,896,256]{3,2,1,0:T(8,128)(2,1)S(1)} collective-permute-done((bf16[2,3,896,256]{3,2,1,0:T(8,128)(2,1)S(1)}, bf16[2,3,896,256]{3,2,1,0:T(8,128)(2,1)S(1)}, u32[]{:S(2)}, u32[]{:S(2)}) %collective-permute-start.11) | collective-permute-done | bytes 2752544 | tf_op jit(solution)/shard_map/ppermute | solution.py:37
  347.0 0.6 collective-permute-start.13
  348.5 0.9 collective-permute-start.12
  349.4 28.0 %collective-permute-done.7.args_5_ = bf16[1,3,896,256]{3,2,1,0:T(8,128)(2,1)} collective-permute-done((bf16[1,3,896,256]{3,2,1,0:T(8,128)(2,1)S(1)}, bf16[1,3,896,256]{3,2,1,0:T(8,128)(2,1)}, u32[]{:S(2)}, u32[]{:S(2)}) %collective-permute-start.7) | collective-permute-done | bytes 1376288 | tf_op jit(solution)/shard_map/ppermute | solution.py:37
  377.5 26.5 %collective-permute-done.13.args_10_ = bf16[1,3,896,256]{3,2,1,0:T(8,128)(2,1)} collective-permute-done((bf16[1,3,896,256]{3,2,1,0:T(8,128)(2,1)S(1)}, bf16[1,3,896,256]{3,2,1,0:T(8,128)(2,1)}, u32[]{:S(2)}, u32[]{:S(2)}) %collective-permute-start.13) | collective-permute-done | bytes 1376288 | tf_op jit(solution)/shard_map/ppermute | solution.py:37
  404.0 27.9 %shard_map.104.args_0_ = bf16[1024,896]{1,0:T(8,128)(2,1)} custom-call(bf16[1024,4096]{1,0:T(8,128)(2,1)} %all-gather.2.cloned.1.call-done.args_0_, bf16[2,3,896,256]{3,2,1,0:T(8,128)(2,1)} %copy-done.2, bf16[2,3,896,256]{3,2,1,0:T(8,128)(2,1)} %copy-done.4, bf16[2,3,896,256]{3,2,1,0:T(8,128)(2,1)} %copy-done.10, ...), custom_call_target="tpu_custom_call" | custom-call | flops 15032385536 | bytes 14680064 | tf_op jit(solution)/shard_map/pallas_call | solution.py:148
  431.9 1.5 copy-done.6
  433.4 21.5 %shard_map.105 = bf16[1024,4096]{1,0:T(8,128)(2,1)} custom-call(bf16[1024,896]{1,0:T(8,128)(2,1)S(1)} %copy-done.6, bf16[2,3,896,256]{3,2,1,0:T(8,128)(2,1)S(1)} %copy-done.3, bf16[2,3,896,256]{3,2,1,0:T(8,128)(2,1)S(1)} %copy-done.5, bf16[2,3,896,256]{3,2,1,0:T(8,128)(2,1)} %copy-done.10, bf16[1,3,896,256]{3,2,1,0:T(8,128)(2,1)} %collective-permute-done.6.args_4_, ...), custom_call_target="tpu_custom_call" | custom-call | flops 7516192768 | bytes 14680064 | tf_op jit(solution)/shard_map/pallas_call | solution.py:163
  454.9 47.4 %reduce-scatter.2.cloned.1.call-done = bf16[1024,2048]{1,0:T(8,128)(2,1)} async-done(((bf16[1024,4096]{1,0:T(8,128)(2,1)}), bf16[1024,2048]{1,0:T(8,128)(2,1)}) %reduce-scatter.2.cloned.1.call-update) | async-done | bytes 4194320 | tf_op jit(solution)/shard_map/reduce_scatter | solution.py:264
  502.3 2.2 fusion.20
  504.5 3.7 collective-permute-start.14
  508.3 1.1 collective-permute-start.15
  509.4 22.5 %collective-permute-done.14 = bf16[256,2048]{1,0:T(8,128)(2,1)S(1)} collective-permute-done((bf16[256,2048]{1,0:T(8,128)(2,1)S(1)}, bf16[256,2048]{1,0:T(8,128)(2,1)S(1)}, u32[]{:S(2)}, u32[]{:S(2)}) %collective-permute-start.14) | collective-permute-done | bytes 1048608 | tf_op jit(solution)/shard_map/ppermute | solution.py:32
  531.8 23.5 %collective-permute-done.16 = bf16[256,2048]{1,0:T(8,128)(2,1)S(1)} collective-permute-done((bf16[256,2048]{1,0:T(8,128)(2,1)S(1)}, bf16[256,2048]{1,0:T(8,128)(2,1)S(1)}, u32[]{:S(2)}, u32[]{:S(2)}) %collective-permute-start.16) | collective-permute-done | bytes 1048608 | tf_op jit(solution)/shard_map/ppermute | solution.py:32
  555.3 43.2 %collective-permute-done.15 = bf16[256,2048]{1,0:T(8,128)(2,1)S(1)} collective-permute-done((bf16[256,2048]{1,0:T(8,128)(2,1)S(1)}, bf16[256,2048]{1,0:T(8,128)(2,1)S(1)}, u32[]{:S(2)}, u32[]{:S(2)}) %collective-permute-start.15) | collective-permute-done | bytes 1048608 | tf_op jit(solution)/shard_map/ppermute | solution.py:32
  598.5 3.1 fusion.8
  (72 shorter events, 4.3 us)
Async XLA Ops:
  7.2 62.6 %copy-start = (bf16[256,128]{1,0:T(8,128)(2,1)S(1)}, bf16[256,128]{1,0:T(8,128)(2,1)}, u32[]{:S(2)}) copy-start(bf16[256,128]{1,0:T(8,128)(2,1)} %param.11) | copy-start | bytes 196612
  9.9 15.5 %all-to-all-start = ((f32[16,1,128]{2,1,0:T(1,128)}), f32[16,1,128]{2,1,0:T(1,128)S(1)}, u32[]{:S(2)}, u32[]{:S(2)}) async-start(f32[16,1,128]{2,1,0:T(1,128)} %all_to_all.12), calls=%async_computation | async-start | bytes 16384 | tf_op jit(solution)/shard_map/all_to_all | solution.py:235
  19.1 1.8 copy-start.15
  25.4 18.2 %all-to-all-start.1 = ((bf16[16,128,128]{2,1,0:T(8,128)(2,1)}), bf16[16,128,128]{2,1,0:T(8,128)(2,1)S(1)}, u32[]{:S(2)}, u32[]{:S(2)}) async-start(bf16[16,128,128]{2,1,0:T(8,128)(2,1)} %bitcast.8), calls=%async_computation.1 | async-start | bytes 1048576 | tf_op jit(solution)/shard_map/all_to_all | solution.py:232
  43.7 1.6 copy-start.13
  65.6 18.9 %copy-start.16 = (f32[32]{0:T(128)S(1)}, f32[32]{0:T(128)}, u32[]{:S(2)}) copy-start(f32[32]{0:T(128)} %param.13) | copy-start | bytes 388
  65.6 18.4 %all-to-all-start.2 = ((bf16[16,128,128]{2,1,0:T(8,128)(2,1)}), bf16[16,128,128]{2,1,0:T(8,128)(2,1)S(1)}, u32[]{:S(2)}, u32[]{:S(2)}) async-start(bf16[16,128,128]{2,1,0:T(8,128)(2,1)} %constant_dynamic-update-slice_fusion), calls=%async_computation.2 | async-start | bytes 1048576 | tf_op jit(solution)/shard_map/all_to_all | solution.py:242
  69.6 334.3 %all-gather.2.cloned.1.call-start = ((), (), s32[]{:S(2)}) async-start(), calls=%async_computation.4 | async-start | bytes 12582912 | tf_op jit(solution)/shard_map/all_gather | solution.py:262
  87.5 3.2 dynamic-slice-start
  90.6 96.0 %copy-start.8 = (bf16[256,2048]{1,0:T(8,128)(2,1)}, bf16[256,2048]{1,0:T(8,128)(2,1)S(1)}, u32[]{:S(2)}) copy-start(bf16[256,2048]{1,0:T(8,128)(2,1)S(1)} %copy.36) | copy-start | bytes 3145732
  90.9 25.5 %collective-permute-start.2 = (bf16[256,2048]{1,0:T(8,128)(2,1)S(1)}, bf16[256,2048]{1,0:T(8,128)(2,1)S(1)}, u32[]{:S(2)}, u32[]{:S(2)}) collective-permute-start(bf16[256,2048]{1,0:T(8,128)(2,1)S(1)} %fusion.7), channel_id=1, source_target_pairs={{0,24},{2,26},{4,28},{6,30},{8,0},{10,2},{12,4},{14,6},{16,8},{18,... | collective-permute-start | bytes 3145736 | tf_op jit(solution)/shard_map/ppermute | solution.py:32
  92.8 91.5 %collective-permute-start.1 = (bf16[256,2048]{1,0:T(8,128)(2,1)S(1)}, bf16[256,2048]{1,0:T(8,128)(2,1)S(1)}, u32[]{:S(2)}, u32[]{:S(2)}) collective-permute-start(bf16[256,2048]{1,0:T(8,128)(2,1)S(1)} %fusion.7), channel_id=1, source_target_pairs={{0,16},{2,18},{4,20},{6,22},{8,24},{10,26},{12,28},{14,30},{16,0},... | collective-permute-start | bytes 3145736 | tf_op jit(solution)/shard_map/ppermute | solution.py:32
  93.7 90.6 %collective-permute-start = (bf16[256,2048]{1,0:T(8,128)(2,1)S(1)}, bf16[256,2048]{1,0:T(8,128)(2,1)S(1)}, u32[]{:S(2)}, u32[]{:S(2)}) collective-permute-start(bf16[256,2048]{1,0:T(8,128)(2,1)S(1)} %fusion.7), channel_id=1, source_target_pairs={{0,8},{2,10},{4,12},{6,14},{8,16},{10,18},{12,20},{14,22},{16,24},... | collective-permute-start | bytes 3145736 | tf_op jit(solution)/shard_map/ppermute | solution.py:32
  186.6 1.5 copy-start.14
  186.6 315.6 %reduce-scatter.2.cloned.1.call-start = ((), (), s32[]{:S(2)}) async-start(), calls=%async_computation.5 | async-start | bytes 12582912 | tf_op jit(solution)/shard_map/reduce_scatter | solution.py:264
  191.7 35.1 %collective-permute-start.3 = (bf16[3,896,256]{2,1,0:T(8,128)(2,1)S(1)}, bf16[3,896,256]{2,1,0:T(8,128)(2,1)S(1)}, u32[]{:S(2)}, u32[]{:S(2)}) collective-permute-start(bf16[3,896,256]{2,1,0:T(8,128)(2,1)S(1)} %get-tuple-element.22), channel_id=1, source_target_pairs={{0,8},{2,10},{4,12},{6,14},{8,16},{10,18},{12,20},{14,22},{16,24},... | collective-permute-start | bytes 4128776 | tf_op jit(solution)/shard_map/ppermute | solution.py:32
  191.8 92.2 %collective-permute-start.8 = (bf16[3,896,256]{2,1,0:T(8,128)(2,1)S(1)}, bf16[3,896,256]{2,1,0:T(8,128)(2,1)S(1)}, u32[]{:S(2)}, u32[]{:S(2)}) collective-permute-start(bf16[3,896,256]{2,1,0:T(8,128)(2,1)S(1)} %get-tuple-element.20), channel_id=1, source_target_pairs={{0,16},{2,18},{4,20},{6,22},{8,24},{10,26},{12,28},{14,30},{16,0},... | collective-permute-start | bytes 4128776 | tf_op jit(solution)/shard_map/ppermute | solution.py:32
  192.9 91.1 %collective-permute-start.9 = (bf16[3,896,256]{2,1,0:T(8,128)(2,1)S(1)}, bf16[3,896,256]{2,1,0:T(8,128)(2,1)S(1)}, u32[]{:S(2)}, u32[]{:S(2)}) collective-permute-start(bf16[3,896,256]{2,1,0:T(8,128)(2,1)S(1)} %get-tuple-element.21), channel_id=1, source_target_pairs={{0,24},{2,26},{4,28},{6,30},{8,0},{10,2},{12,4},{14,6},{16,8},{18,... | collective-permute-start | bytes 4128776 | tf_op jit(solution)/shard_map/ppermute | solution.py:32
  227.0 57.2 %copy-start.2 = (bf16[2,3,896,256]{3,2,1,0:T(8,128)(2,1)}, bf16[2,3,896,256]{3,2,1,0:T(8,128)(2,1)S(1)}, u32[]{:S(2)}) copy-start(bf16[2,3,896,256]{3,2,1,0:T(8,128)(2,1)S(1)} %pad_maximum_fusion.2.args_1_) | copy-start | bytes 8257540
  227.0 58.8 %collective-permute-start.5 = (bf16[2,3,896,256]{3,2,1,0:T(8,128)(2,1)S(1)}, bf16[2,3,896,256]{3,2,1,0:T(8,128)(2,1)S(1)}, u32[]{:S(2)}, u32[]{:S(2)}) collective-permute-start(bf16[2,3,896,256]{3,2,1,0:T(8,128)(2,1)S(1)} %pad_maximum_fusion.2.args_1_), channel_id=1, source_target_pairs={{0,4},{2,6},{4,0},{6,2},{8,12},{10,14},{12,8},{14,10},{16,20},{18,... | collective-permute-start | bytes 8257544 | tf_op jit(solution)/shard_map/ppermute | solution.py:37
  227.8 59.6 %collective-permute-start.4 = (bf16[2,3,896,256]{3,2,1,0:T(8,128)(2,1)S(1)}, bf16[2,3,896,256]{3,2,1,0:T(8,128)(2,1)S(1)}, u32[]{:S(2)}, u32[]{:S(2)}) collective-permute-start(bf16[2,3,896,256]{3,2,1,0:T(8,128)(2,1)S(1)} %pad_maximum_fusion.2.args_1_), channel_id=1, source_target_pairs={{0,2},{2,0},{4,6},{6,4},{8,10},{10,8},{12,14},{14,12},{16,18},{18,... | collective-permute-start | bytes 8257544 | tf_op jit(solution)/shard_map/ppermute | solution.py:37
  284.2 3.3 copy-start.7
  284.3 62.7 %collective-permute-start.11 = (bf16[2,3,896,256]{3,2,1,0:T(8,128)(2,1)S(1)}, bf16[2,3,896,256]{3,2,1,0:T(8,128)(2,1)S(1)}, u32[]{:S(2)}, u32[]{:S(2)}) collective-permute-start(bf16[2,3,896,256]{3,2,1,0:T(8,128)(2,1)S(1)} %pad_maximum_fusion.3.args_6_), channel_id=1, source_target_pairs={{0,4},{2,6},{4,0},{6,2},{8,12},{10,14},{12,8},{14,10},{16,20},{18,... | collective-permute-start | bytes 8257544 | tf_op jit(solution)/shard_map/ppermute | solution.py:37
  285.2 62.6 %collective-permute-start.10 = (bf16[2,3,896,256]{3,2,1,0:T(8,128)(2,1)S(1)}, bf16[2,3,896,256]{3,2,1,0:T(8,128)(2,1)S(1)}, u32[]{:S(2)}, u32[]{:S(2)}) collective-permute-start(bf16[2,3,896,256]{3,2,1,0:T(8,128)(2,1)S(1)} %pad_maximum_fusion.3.args_6_), channel_id=1, source_target_pairs={{0,2},{2,0},{4,6},{6,4},{8,10},{10,8},{12,14},{14,12},{16,18},{18,... | collective-permute-start | bytes 8257544 | tf_op jit(solution)/shard_map/ppermute | solution.py:37
  285.8 1.7 copy-start.10
  285.9 91.6 %collective-permute-start.7 = (bf16[1,3,896,256]{3,2,1,0:T(8,128)(2,1)S(1)}, bf16[1,3,896,256]{3,2,1,0:T(8,128)(2,1)}, u32[]{:S(2)}, u32[]{:S(2)}) collective-permute-start(bf16[1,3,896,256]{3,2,1,0:T(8,128)(2,1)S(1)} %slice.258), channel_id=1, source_target_pairs={{0,2},{2,0},{4,6},{6,4},{8,10},{10,8},{12,14},{14,12},{16,18},{18,... | collective-permute-start | bytes 4128776 | tf_op jit(solution)/shard_map/ppermute | solution.py:37
  287.4 59.6 %copy-start.4 = (bf16[2,3,896,256]{3,2,1,0:T(8,128)(2,1)}, bf16[2,3,896,256]{3,2,1,0:T(8,128)(2,1)S(1)}, u32[]{:S(2)}) copy-start(bf16[2,3,896,256]{3,2,1,0:T(8,128)(2,1)S(1)} %collective-permute-done.4.args_2_) | copy-start | bytes 8257540
  287.6 89.9 %collective-permute-start.6 = (bf16[1,3,896,256]{3,2,1,0:T(8,128)(2,1)S(1)}, bf16[1,3,896,256]{3,2,1,0:T(8,128)(2,1)}, u32[]{:S(2)}, u32[]{:S(2)}) collective-permute-start(bf16[1,3,896,256]{3,2,1,0:T(8,128)(2,1)S(1)} %slice.257), channel_id=1, source_target_pairs={{0,4},{2,6},{4,0},{6,2},{8,12},{10,14},{12,8},{14,10},{16,20},{18,... | collective-permute-start | bytes 4128776 | tf_op jit(solution)/shard_map/ppermute | solution.py:37
  346.9 1.5 copy-start.11
  347.0 56.9 %collective-permute-start.13 = (bf16[1,3,896,256]{3,2,1,0:T(8,128)(2,1)S(1)}, bf16[1,3,896,256]{3,2,1,0:T(8,128)(2,1)}, u32[]{:S(2)}, u32[]{:S(2)}) collective-permute-start(bf16[1,3,896,256]{3,2,1,0:T(8,128)(2,1)S(1)} %slice.260), channel_id=1, source_target_pairs={{0,2},{2,0},{4,6},{6,4},{8,10},{10,8},{12,14},{14,12},{16,18},{18,... | collective-permute-start | bytes 4128776 | tf_op jit(solution)/shard_map/ppermute | solution.py:37
  347.9 1.6 copy-start.12
  348.5 83.4 %copy-start.3 = (bf16[2,3,896,256]{3,2,1,0:T(8,128)(2,1)S(1)}, bf16[2,3,896,256]{3,2,1,0:T(8,128)(2,1)}, u32[]{:S(2)}) copy-start(bf16[2,3,896,256]{3,2,1,0:T(8,128)(2,1)} %copy-done.2) | copy-start | bytes 8257540
  348.5 55.5 %collective-permute-start.12 = (bf16[1,3,896,256]{3,2,1,0:T(8,128)(2,1)S(1)}, bf16[1,3,896,256]{3,2,1,0:T(8,128)(2,1)}, u32[]{:S(2)}, u32[]{:S(2)}) collective-permute-start(bf16[1,3,896,256]{3,2,1,0:T(8,128)(2,1)S(1)} %slice.259), channel_id=1, source_target_pairs={{0,4},{2,6},{4,0},{6,2},{8,12},{10,14},{12,8},{14,10},{16,20},{18,... | collective-permute-start | bytes 4128776 | tf_op jit(solution)/shard_map/ppermute | solution.py:37
  404.0 27.9 %copy-start.5 = (bf16[2,3,896,256]{3,2,1,0:T(8,128)(2,1)S(1)}, bf16[2,3,896,256]{3,2,1,0:T(8,128)(2,1)}, u32[]{:S(2)}) copy-start(bf16[2,3,896,256]{3,2,1,0:T(8,128)(2,1)} %copy-done.4) | copy-start | bytes 8257540
  431.9 1.5 copy-start.6
  454.9 143.7 %copy-start.9 = (bf16[256,2048]{1,0:T(8,128)(2,1)S(1)}, bf16[256,2048]{1,0:T(8,128)(2,1)}, u32[]{:S(2)}) copy-start(bf16[256,2048]{1,0:T(8,128)(2,1)} %copy-done.8) | copy-start | bytes 3145732
  504.5 27.3 %collective-permute-start.14 = (bf16[256,2048]{1,0:T(8,128)(2,1)S(1)}, bf16[256,2048]{1,0:T(8,128)(2,1)S(1)}, u32[]{:S(2)}, u32[]{:S(2)}) collective-permute-start(bf16[256,2048]{1,0:T(8,128)(2,1)S(1)} %get-tuple-element.24), channel_id=1, source_target_pairs={{0,24},{2,26},{4,28},{6,30},{8,0},{10,2},{12,4},{14,6},{16,8},{18,... | collective-permute-start | bytes 3145736 | tf_op jit(solution)/shard_map/ppermute | solution.py:32
  508.3 47.1 %collective-permute-start.16 = (bf16[256,2048]{1,0:T(8,128)(2,1)S(1)}, bf16[256,2048]{1,0:T(8,128)(2,1)S(1)}, u32[]{:S(2)}, u32[]{:S(2)}) collective-permute-start(bf16[256,2048]{1,0:T(8,128)(2,1)S(1)} %get-tuple-element.25), channel_id=1, source_target_pairs={{0,8},{2,10},{4,12},{6,14},{8,16},{10,18},{12,20},{14,22},{16,24},... | collective-permute-start | bytes 3145736 | tf_op jit(solution)/shard_map/ppermute | solution.py:32
  508.3 93.4 %copy-start.1 = (bf16[256,128]{1,0:T(8,128)(2,1)S(1)}, bf16[256,128]{1,0:T(8,128)(2,1)}, u32[]{:S(2)}) copy-start(bf16[256,128]{1,0:T(8,128)(2,1)} %param.11) | copy-start | bytes 196612
  508.3 90.3 %collective-permute-start.15 = (bf16[256,2048]{1,0:T(8,128)(2,1)S(1)}, bf16[256,2048]{1,0:T(8,128)(2,1)S(1)}, u32[]{:S(2)}, u32[]{:S(2)}) collective-permute-start(bf16[256,2048]{1,0:T(8,128)(2,1)S(1)} %get-tuple-element.26), channel_id=1, source_target_pairs={{0,16},{2,18},{4,20},{6,22},{8,24},{10,26},{12,28},{14,30},{16,0},... | collective-permute-start | bytes 3145736 | tf_op jit(solution)/shard_map/ppermute | solution.py:32
Sparse Core Ops, SparseCore 0:
  186.8 17.6 all-gather.1
  455.0 47.2 reduce-scatter.1

commit v2 on v1

--- a/solution.py
+++ b/solution.py
@@ -52,7 +52,7 @@
     count = 5 * major // 2
     x_ref, w_refs = args[0], args[1 : 1 + count]
     h_ref, wbuf, acc, sem = args[1 + count :]
-    rows = x_ref.shape[0]
+    _, rows, width = x_ref.shape
     tile = min(rows, 256)
     me = lax.axis_index("seq")
     a, b = me // MINOR, me % MINOR
@@ -74,17 +74,14 @@
         for c in fetch(k):
             c.wait()
         src = (a + major - k) % major
-        cols = [
-            pl.ds(pl.multiple_of((src * MINOR + flip(b, m)) * depth, depth), depth)
-            for m in range(MINOR)
-        ]
+        starts = [(src * MINOR + flip(b, m)) * depth for m in range(MINOR)]
 
         @pl.loop(0, rows // tile)
         def _(i):
             at = pl.ds(pl.multiple_of(i * tile, tile), tile)
             sums = [None, None]
             for m in range(MINOR):
-                x = x_ref[at, cols[m]]
+                x = x_ref[starts[m] // width, at, pl.ds(pl.multiple_of(starts[m] % width, depth), depth)]
                 for q in range(2):
                     d = nt(x, wbuf[k % 2, m, q])
                     sums[q] = d if sums[q] is None else sums[q] + d
@@ -103,6 +100,7 @@
     h_ref, w_refs = args[0], args[1 : 1 + count]
     o_ref, wbuf, obuf, sem, osem = args[1 + count :]
     rows = h_ref.shape[0]
+    width = o_ref.shape[2]
     tile = min(rows, 256)
     me = lax.axis_index("seq")
     a, b = me // MINOR, me % MINOR
@@ -115,8 +113,11 @@
     def put(j):
         k, m = steps[j]
         src = (a + major - k) % major
-        col = pl.multiple_of((src * MINOR + flip(b, m)) * depth, depth)
-        return pltpu.make_async_copy(obuf.at[j % 2], o_ref.at[:, pl.ds(col, depth)], osem.at[j % 2])
+        start = (src * MINOR + flip(b, m)) * depth
+        col = pl.ds(pl.multiple_of(start % width, depth), depth)
+        return pltpu.make_async_copy(
+            obuf.at[j % 2], o_ref.at[start // width, :, col], osem.at[j % 2]
+        )
 
     fetch(0).start()
     for j in range(len(steps)):
@@ -138,12 +139,21 @@
     put(len(steps) - 1).wait()
 
 
+def prefix_kernel(finals_ref, decay_ref, o_ref):
+    n, rows, states = o_ref.shape
+    state = jnp.zeros((rows, states), F32)
+    for j in range(n):
+        o_ref[j] = state.astype(BF)
+        state = decay_ref[j] * state + finals_ref[j, pl.ds(0, rows), :].astype(F32)
+
+
 ANY = pl.BlockSpec(memory_space=pl.ANY)
 INV = pl.BlockSpec(memory_space=pltpu.VMEM)
 
 
 def feed_forward(normed, pieces, major, depth):
-    rows, width = normed.shape
+    shares, rows, share = normed.shape
+    width = shares * share
     units = pieces[0].shape[2]
     hidden = pl.pallas_call(
         functools.partial(gate_up_kernel, major, depth),
@@ -162,7 +172,7 @@
     )(normed, *pieces)
     return pl.pallas_call(
         functools.partial(down_kernel, major, depth),
-        out_shape=jax.ShapeDtypeStruct((rows, width), BF),
+        out_shape=jax.ShapeDtypeStruct(normed.shape, BF),
         in_specs=[INV] + [ANY] * len(pieces),
         out_specs=ANY,
         scratch_shapes=[
@@ -176,6 +186,24 @@
             flops=2 * rows * units * width, bytes_accessed=4 * units * width, transcendentals=0
         ),
     )(hidden, *pieces)
+
+
+def share_features(x):
+    if lax.axis_size("tp") != 2:
+        return lax.all_gather(x, "tp", axis=1, tiled=True)[None]
+    other = lax.ppermute(x, "tp", [(0, 1), (1, 0)])
+    first = lax.axis_index("tp") == 0
+    return jnp.stack([jnp.where(first, x, other), jnp.where(first, other, x)])
+
+
+def own_features(partial):
+    if lax.axis_size("tp") != 2:
+        return lax.psum_scatter(partial[0], "tp", scatter_dimension=1, tiled=True)
+    t = lax.axis_index("tp")
+    give = lax.dynamic_index_in_dim(partial, 1 - t, axis=0, keepdims=False)
+    keep = lax.dynamic_index_in_dim(partial, t, axis=0, keepdims=False)
+    come = lax.ppermute(give, "tp", [(0, 1), (1, 0)])
+    return (keep.astype(F32) + come.astype(F32)).astype(BF)
 
 
 def on_device(
@@ -207,14 +235,6 @@
         return lax.dynamic_index_in_dim(stacked, (a + k) % major, axis=1, keepdims=False)
 
     got = [chunk(0)] + [along_major(chunk(k), k, n) for k in range(1, major)]
-    pieces = []
-    for g in range(0, major, 2):
-        own = jnp.stack(got[g : g + 2])
-        over_x = along_minor(own, 1, n)
-        over_y = along_minor(own, 2, n)
-        first = along_minor(over_x[:1], 2, n)
-        second = along_minor(over_y[1:], 1, n)
-        pieces += [own, over_x, over_y, first, second]
 
     x = ssm_inputs.astype(F32).reshape(toks, heads, hdim)
     scaled = x * jnp.sqrt(-jnp.expm1(2.0 * log_decay))[:, :, None]
@@ -228,18 +248,30 @@
         preferred_element_type=F32,
     )
     rows = feats // n
-    row_total = jnp.repeat(total, hdim).reshape(n, rows)
-    finals = lax.all_to_all(
-        local_final.astype(BF).reshape(n, rows, states), "seq", 0, 0, tiled=True
-    ).astype(F32)
-    decays = jnp.exp(lax.all_to_all(row_total, "seq", 0, 0, tiled=True))
-    state = jnp.zeros((rows, states), F32)
-    before = []
-    for j in range(n):
-        before.append(state.astype(BF))
-        if j + 1 < n:
-            state = decays[j][:, None] * state + finals[j]
-    incoming = lax.all_to_all(jnp.stack(before), "seq", 0, 0, tiled=True).reshape(feats, states)
+    decay = jnp.repeat(jnp.exp(total), hdim).reshape(n, 1, rows)
+    high = decay.astype(BF)
+    low = (decay - high.astype(F32)).astype(BF)
+    extra = jnp.concatenate([high, low, jnp.zeros((n, 14, rows), BF)], axis=1)
+    extra = jnp.pad(extra, ((0, 0), (0, 0), (0, states - rows)))
+    payload = jnp.concatenate([local_final.astype(BF).reshape(n, rows, states), extra], axis=1)
+    finals = lax.all_to_all(payload, "seq", 0, 0, tiled=True)
+    decays = finals[:, rows, :rows].astype(F32) + finals[:, rows + 1, :rows].astype(F32)
+    before = pl.pallas_call(
+        prefix_kernel,
+        out_shape=jax.ShapeDtypeStruct((n, rows, states), BF),
+        in_specs=[INV, INV],
+        out_specs=INV,
+    )(finals, decays[:, :, None])
+    before, got[1] = lax.optimization_barrier((before, got[1]))
+    incoming = lax.all_to_all(before, "seq", 0, 0, tiled=True).reshape(feats, states)
+    incoming, *got[2:] = lax.optimization_barrier((incoming, *got[2:]))
+
+    def first_hops(g):
+        own = jnp.stack(got[g : g + 2])
+        return [own, along_minor(own, 1, n), along_minor(own, 2, n)]
+
+    def second_hops(hops):
+        return [along_minor(hops[1][:1], 2, n), along_minor(hops[2][1:], 1, n)]
 
     scores = nt(read_proj, write_proj)
     r = running.T
@@ -258,14 +290,26 @@
     gain = lax.dynamic_slice_in_dim(norm_gain, lax.axis_index("tp") * feats, feats)
     normed = (rows_f * lax.rsqrt(square_sum / (feats * tp) + 1e-05) * gain[None, :]).astype(BF)
 
-    group = jnp.concatenate([normed] + [along_major(normed, k, n) for k in range(1, major)], axis=0)
-    group = lax.all_gather(group, "tp", axis=1, tiled=True)
-    partial = feed_forward(group, pieces, major, depth)
-    own = lax.psum_scatter(partial, "tp", scatter_dimension=1, tiled=True)
-    own = own.reshape(major, toks, feats)
-    mlp = own[0].astype(F32)
-    for k in range(1, major):
-        mlp = mlp + along_major(own[k], major - k, n).astype(F32)
+    groups = [first_hops(g) for g in range(0, major, 2)]
+    normed, groups[0] = lax.optimization_barrier((normed, groups[0]))
+    tokens = [normed] + [along_major(normed, k, n) for k in range(1, major)]
+    cut = major // 2 + 1
+    pieces = groups[0] + second_hops(groups[0])
+    tokens[1:cut], groups[1:], pieces = lax.optimization_barrier(
+        (tokens[1:cut], groups[1:], pieces)
+    )
+    pieces = pieces + sum([g + second_hops(g) for g in groups[1:]], [])
+
+    order = list(range(1, major)) + [0]
+    backs = []
+    for half in (order[: major // 2], order[major // 2 :]):
+        some = jnp.concatenate([tokens[k] for k in half], axis=0)
+        partial = feed_forward(share_features(some), pieces, major, depth)
+        if backs:
+            partial, backs = lax.optimization_barrier((partial, backs))
+        own = own_features(partial).reshape(len(half), toks, feats)
+        backs += [along_major(own[i], major - k, n) if k else own[i] for i, k in enumerate(half)]
+    mlp = sum(back.astype(F32) for back in backs)
     mixed = (rows_f + mlp).astype(BF)
     return (ssd_out, mixed)
 

time: 610 us -> 469 us (0.77)
  waiting for transfers between devices: 458 us -> 222 us
  starting transfers between devices: 34.8 us -> 117 us
  local copies, waits for them, and re-layouts: 11.2 us -> 31.2 us
  between operations: 14.5 us -> 1.15 us
  Pallas kernels: 49.4 us -> 59.6 us
    ppermute x9, waiting for transfers between devices: 266 us -> 101 us  [along_major(): return lax.ppermute(x, 'seq', route)]
    all_to_all x3 -> x2, starting transfers between devices: 15.9 us -> 71.3 us  [the longest x1 65.5 us: on_device(): lax.all_to_all(before, 'seq', 0, 0, tiled=True).reshape(feats, states)]
    reduce_scatter x1 -> x0, waiting for transfers between devices: 47.4 us -> none  [on_device(): own = lax.psum_scatter(partial, 'tp', scatter_dimension=1, tiled=True)]
    ppermute x8, waiting for transfers between devices: 113 us -> 81.7 us  [along_minor(): return lax.ppermute(x, 'seq', route)]
    ppermute x9, starting transfers between devices: 11.6 us -> 36.6 us  [along_major(): return lax.ppermute(x, 'seq', route)]
    unnamed x14 -> x0, other arithmetic: 20.3 us -> none
    another operation x6 -> x9, other arithmetic: 2.73 us -> 16.2 us  [the longest x4 9.29 us: share_features(): return jnp.stack([jnp.where(first, x, other), jnp.where(first, other, x)])]
    unnamed x37 -> x56, local copies, waits for them, and re-layouts: 6.2 us -> 12.4 us
  transfers between devices with their start and end apart: 22 -> 23, of which waited for: 15 -> 16; matrix products, arithmetic and copies ran while one was open for 1% -> 10% of each run, Pallas kernels for 0% -> 13%
where the time goes in v2:
time: 469 us; the launch traced here: 468 us
  waiting for transfers between devices  222 us (47%)
  starting transfers between devices  117 us (25%)
  Pallas kernels  59.6 us (13%)
  local copies, waits for them, and re-layouts  31.2 us (7%)
  other arithmetic  30.5 us (7%)
    ppermute x9, waiting for transfers between devices, along_major(): return lax.ppermute(x, 'seq', route)  101 us
    ppermute x8, waiting for transfers between devices, along_minor(): return lax.ppermute(x, 'seq', route)  81.7 us
    all_to_all x1, starting transfers between devices, on_device(): lax.all_to_all(before, 'seq', 0, 0, tiled=True).reshape(feats, states)  65.5 us
    ppermute x9, starting transfers between devices, along_major(): return lax.ppermute(x, 'seq', route)  36.6 us
    pallas_call x2, Pallas kernels, feed_forward(): pl.pallas_call(functools.partial(gate_up_kernel, major, depth), out_shape...  31.4 us
    all_to_all x1, waiting for transfers between devices, on_device(): finals = lax.all_to_all(payload, 'seq', 0, 0, tiled=True)  28.8 us
    pallas_call x2, Pallas kernels, feed_forward(): pl.pallas_call(functools.partial(down_kernel, major, depth), out_shape=ja...  25.6 us
    unnamed x56, local copies, waits for them, and re-layouts  12.4 us
  transfers between devices with their start and end apart: 23, of which 16 were waited for; matrix products, arithmetic and copies ran while one was open for 10% of the time, Pallas kernels for 13%

profile of v2, /device:TPU:0, one launch (start us, length us, event | category | flops | bytes accessed | tf_op | source)
XLA Modules:
  0.0 468.0 jit_solution(16275958489752601471)
XLA Ops:
  0.7 3.4 pad_maximum_fusion
  4.2 2.1 dynamic-slice_bitcast_fusion.2
  6.3 3.0 collective-permute-start
  12.6 1.1 fusion.11
  14.2 1.0 maximum_maximum_fusion
  15.2 5.9 %all-to-all-start = ((bf16[16,144,128]{2,1,0:T(8,128)(2,1)}), bf16[16,144,128]{2,1,0:T(8,128)(2,1)S(1)}, u32[]{:S(2)}, u32[]{:S(2)}) async-start(bf16[16,144,128]{2,1,0:T(8,128)(2,1)} %maximum_maximum_fusion), calls=%async_computation | async-start | bytes 1179648 | tf_op jit(solution)/shard_map/all_to_all | solution.py:257
  21.1 3.7 collective-permute-start.2
  24.8 28.8 %all-to-all-done.finals_ref = bf16[16,144,128]{2,1,0:T(8,128)(2,1)S(1)} async-done(((bf16[16,144,128]{2,1,0:T(8,128)(2,1)}), bf16[16,144,128]{2,1,0:T(8,128)(2,1)S(1)}, u32[]{:S(2)}, u32[]{:S(2)}) %all-to-all-start) | async-done | bytes 589856 | tf_op jit(solution)/shard_map/all_to_all | solution.py:257
  53.7 1.3 copy.34.decay_ref
  55.0 2.5 shard_map.104
  57.6 65.5 %all-to-all-start.1 = ((bf16[16,128,128]{2,1,0:T(8,128)(2,1)}), bf16[16,128,128]{2,1,0:T(8,128)(2,1)S(1)}, u32[]{:S(2)}, u32[]{:S(2)}) async-start(bf16[16,128,128]{2,1,0:T(8,128)(2,1)} %shard_map.104), calls=%async_computation.1 | async-start | bytes 1048576 | tf_op jit(solution)/shard_map/all_to_all | solution.py:266
  123.0 2.0 pad_maximum_fusion.3.args_1_
  125.1 2.0 collective-permute-start.4
  127.0 1.5 collective-permute-start.3
  128.5 20.2 %collective-permute-done.1 = bf16[3,896,256]{2,1,0:T(8,128)(2,1)} collective-permute-done((bf16[3,896,256]{2,1,0:T(8,128)(2,1)}, bf16[3,896,256]{2,1,0:T(8,128)(2,1)}, u32[]{:S(2)}, u32[]{:S(2)}) %collective-permute-start.1) | collective-permute-done | bytes 1376288 | tf_op jit(solution)/shard_map/ppermute | solution.py:32
  148.7 5.4 %all-to-all-done.1 = bf16[16,128,128]{2,1,0:T(8,128)(2,1)S(1)} async-done(((bf16[16,128,128]{2,1,0:T(8,128)(2,1)}), bf16[16,128,128]{2,1,0:T(8,128)(2,1)S(1)}, u32[]{:S(2)}, u32[]{:S(2)}) %all-to-all-start.1) | async-done | bytes 524320 | tf_op jit(solution)/shard_map/all_to_all | solution.py:266
  154.1 3.6 pad_maximum_fusion.4.args_6_
  157.7 1.2 collective-permute-start.10
  159.2 3.4 fusion
  163.8 1.9 multiply_reduce_fusion
  165.7 2.3 copy.39
  168.0 2.4 psum.7
  170.4 2.5 fusion.9
  172.9 18.5 %collective-permute-done.4.args_3_ = bf16[2,3,896,256]{3,2,1,0:T(8,128)(2,1)} collective-permute-done((bf16[2,3,896,256]{3,2,1,0:T(8,128)(2,1)S(1)}, bf16[2,3,896,256]{3,2,1,0:T(8,128)(2,1)}, u32[]{:S(2)}, u32[]{:S(2)}) %collective-permute-start.4) | collective-permute-done | bytes 2752544 | tf_op jit(solution)/shard_map/ppermute | solution.py:37
  191.4 1.3 collective-permute-done.3.args_2_
  192.7 1.4 slice.48
  194.2 1.4 slice.49
  195.6 1.3 collective-permute-start.12
  197.6 1.6 collective-permute-start.8
  199.2 51.2 %collective-permute-done.10.args_8_ = bf16[2,3,896,256]{3,2,1,0:T(8,128)(2,1)} collective-permute-done((bf16[2,3,896,256]{3,2,1,0:T(8,128)(2,1)}, bf16[2,3,896,256]{3,2,1,0:T(8,128)(2,1)}, u32[]{:S(2)}, u32[]{:S(2)}) %collective-permute-start.10) | collective-permute-done | bytes 2752544 | tf_op jit(solution)/shard_map/ppermute | solution.py:37
  250.4 1.2 collective-permute-start.7
  251.7 20.8 %collective-permute-done.7 = bf16[256,2048]{1,0:T(8,128)(2,1)S(1)} collective-permute-done((bf16[256,2048]{1,0:T(8,128)(2,1)}, bf16[256,2048]{1,0:T(8,128)(2,1)S(1)}, u32[]{:S(2)}, u32[]{:S(2)}) %collective-permute-start.7) | collective-permute-done | bytes 1048608 | tf_op jit(solution)/shard_map/ppermute | solution.py:32
  272.5 6.3 %collective-permute-done.12.args_5_ = bf16[1,3,896,256]{3,2,1,0:T(8,128)(2,1)} collective-permute-done((bf16[1,3,896,256]{3,2,1,0:T(8,128)(2,1)S(1)}, bf16[1,3,896,256]{3,2,1,0:T(8,128)(2,1)}, u32[]{:S(2)}, u32[]{:S(2)}) %collective-permute-start.12) | collective-permute-done | bytes 1376288 | tf_op jit(solution)/shard_map/ppermute | solution.py:37
  279.1 3.1 collective-permute-start.5
  282.2 1.4 slice.50
  283.6 1.4 slice.51
  285.6 1.2 collective-permute-start.13
  286.8 18.5 %collective-permute-done.5 = bf16[256,2048]{1,0:T(8,128)(2,1)S(1)} collective-permute-done((bf16[256,2048]{1,0:T(8,128)(2,1)}, bf16[256,2048]{1,0:T(8,128)(2,1)S(1)}, u32[]{:S(2)}, u32[]{:S(2)}) %collective-permute-start.5) | collective-permute-done | bytes 1048608 | tf_op jit(solution)/shard_map/ppermute | solution.py:32
  305.3 1.0 constant_dynamic-update-slice_fusion.1
  306.4 2.4 constant_dynamic-update-slice_fusion
  308.8 1.9 select_bitcast_fusion.1
  310.7 2.4 pad_maximum_fusion.2.args_0_
  313.1 4.1 collective-permute-done.14.args_10_
  318.3 1.1 copy-done.8
  319.4 15.7 %shard_map.107.args_0_ = bf16[512,896]{1,0:T(8,128)(2,1)} custom-call(bf16[2,512,2048]{2,1,0:T(8,128)(2,1)} %pad_maximum_fusion.2.args_0_, bf16[2,3,896,256]{3,2,1,0:T(8,128)(2,1)} %copy-done.2, bf16[2,3,896,256]{3,2,1,0:T(8,128)(2,1)} %collective-permute-done.3.args_2_, bf16[2,3,896,256]{3,2,1,0:T(8,128)(2,1)} %collective-permute-done.4.args_3_, ...), custom_call_target="tpu_custom_call" | custom-call | flops 7516192768 | bytes 14680064 | tf_op jit(solution)/shard_map/pallas_call | solution.py:158
  335.1 1.3 copy-done.6
  336.4 1.3 copy-done.9
  337.8 1.2 copy-done.12
  338.9 12.8 %shard_map.108 = bf16[2,512,2048]{2,1,0:T(8,128)(2,1)} custom-call(bf16[512,896]{1,0:T(8,128)(2,1)S(1)} %copy-done.12, bf16[2,3,896,256]{3,2,1,0:T(8,128)(2,1)S(1)} %copy-done.3, bf16[2,3,896,256]{3,2,1,0:T(8,128)(2,1)} %collective-permute-done.3.args_2_, bf16[2,3,896,256]{3,2,1,0:T(8,128)(2,1)} %collective-permute-done.4.args_3_, ...), custom_call_target="tpu_custom_call" | custom-call | flops 3758096384 | bytes 14680064 | tf_op jit(solution)/shard_map/pallas_call | solution.py:173
  351.7 3.2 dynamic-slice_bitcast_fusion.1
  354.9 2.5 select_bitcast_fusion.3
  357.4 2.5 pad_maximum_fusion.1.args_0_
  360.0 1.2 copy-done.13
  361.9 1.5 fusion.21
  363.4 1.6 collective-permute-start.17
  365.0 15.7 %shard_map.105.args_0_ = bf16[512,896]{1,0:T(8,128)(2,1)} custom-call(bf16[2,512,2048]{2,1,0:T(8,128)(2,1)} %pad_maximum_fusion.1.args_0_, bf16[2,3,896,256]{3,2,1,0:T(8,128)(2,1)} %copy-done.2, bf16[2,3,896,256]{3,2,1,0:T(8,128)(2,1)} %collective-permute-done.3.args_2_, bf16[2,3,896,256]{3,2,1,0:T(8,128)(2,1)} %collective-permute-done.4.args_3_, ...), custom_call_target="tpu_custom_call" | custom-call | flops 7516192768 | bytes 14680064 | tf_op jit(solution)/shard_map/pallas_call | solution.py:158
  380.8 1.2 copy-done.11
  382.0 12.8 %shard_map.106 = bf16[2,512,2048]{2,1,0:T(8,128)(2,1)} custom-call(bf16[512,896]{1,0:T(8,128)(2,1)S(1)} %copy-done.11, bf16[2,3,896,256]{3,2,1,0:T(8,128)(2,1)S(1)} %copy-done.4, bf16[2,3,896,256]{3,2,1,0:T(8,128)(2,1)} %collective-permute-done.3.args_2_, bf16[2,3,896,256]{3,2,1,0:T(8,128)(2,1)} %collective-permute-done.4.args_3_, ...), custom_call_target="tpu_custom_call" | custom-call | flops 3758096384 | bytes 14680064 | tf_op jit(solution)/shard_map/pallas_call | solution.py:173
  394.8 16.5 %collective-permute-done.18 = bf16[256,2048]{1,0:T(8,128)(2,1)S(1)} collective-permute-done((bf16[256,2048]{1,0:T(8,128)(2,1)}, bf16[256,2048]{1,0:T(8,128)(2,1)S(1)}, u32[]{:S(2)}, u32[]{:S(2)}) %collective-permute-start.18) | collective-permute-done | bytes 1048608 | tf_op jit(solution)/shard_map/ppermute | solution.py:32
  411.9 1.7 dynamic-slice_bitcast_fusion
  413.8 4.1 collective-permute-done.19
  418.9 22.4 %collective-permute-start.20 = (bf16[256,2048]{1,0:T(8,128)(2,1)S(1)}, bf16[256,2048]{1,0:T(8,128)(2,1)S(1)}, u32[]{:S(2)}, u32[]{:S(2)}) collective-permute-start(bf16[256,2048]{1,0:T(8,128)(2,1)S(1)} %slice.62), channel_id=1, source_target_pairs={{0,8},{2,10},{4,12},{6,14},{8,16},{10,18},{12,20},{14,22},{16,24},... | collective-permute-start | bytes 3145736 | tf_op jit(solution)/shard_map/ppermute | solution.py:32
  441.3 24.8 %collective-permute-done.20 = bf16[256,2048]{1,0:T(8,128)(2,1)S(1)} collective-permute-done((bf16[256,2048]{1,0:T(8,128)(2,1)S(1)}, bf16[256,2048]{1,0:T(8,128)(2,1)S(1)}, u32[]{:S(2)}, u32[]{:S(2)}) %collective-permute-start.20) | collective-permute-done | bytes 1048608 | tf_op jit(solution)/shard_map/ppermute | solution.py:32
  466.1 1.9 fusion.10
  (93 shorter events, 10.6 us)
Async XLA Ops:
  0.6 158.3 %copy-start = (bf16[256,128]{1,0:T(8,128)(2,1)S(1)}, bf16[256,128]{1,0:T(8,128)(2,1)}, u32[]{:S(2)}) copy-start(bf16[256,128]{1,0:T(8,128)(2,1)} %param.11) | copy-start | bytes 196612
  4.2 5.1 %copy-start.23 = (f32[256,32]{0,1:T(8,128)S(1)}, f32[256,32]{0,1:T(8,128)}, u32[]{:S(2)}) copy-start(f32[256,32]{0,1:T(8,128)} %param.12) | copy-start | bytes 98308
  4.2 7.8 %copy-start.19 = (bf16[256,2048]{1,0:T(8,128)(2,1)S(1)}, bf16[256,2048]{1,0:T(8,128)(2,1)}, u32[]{:S(2)}) copy-start(bf16[256,2048]{1,0:T(8,128)(2,1)} %param.9) | copy-start | bytes 3145732
  6.3 51.3 %collective-permute-start = (bf16[3,896,256]{2,1,0:T(8,128)(2,1)S(1)}, bf16[3,896,256]{2,1,0:T(8,128)(2,1)}, u32[]{:S(2)}, u32[]{:S(2)}) collective-permute-start(bf16[3,896,256]{2,1,0:T(8,128)(2,1)S(1)} %get-tuple-element.57), channel_id=1, source_target_pairs={{0,8},{2,10},{4,12},{6,14},{8,16},{10,18},{12,20},{14,22},{16,24},... | collective-permute-start | bytes 4128776 | tf_op jit(solution)/shard_map/ppermute | solution.py:32
  12.5 2.7 copy-start.16
  12.5 1.3 copy-start.20
  15.2 38.4 %all-to-all-start = ((bf16[16,144,128]{2,1,0:T(8,128)(2,1)}), bf16[16,144,128]{2,1,0:T(8,128)(2,1)S(1)}, u32[]{:S(2)}, u32[]{:S(2)}) async-start(bf16[16,144,128]{2,1,0:T(8,128)(2,1)} %maximum_maximum_fusion), calls=%async_computation | async-start | bytes 1179648 | tf_op jit(solution)/shard_map/all_to_all | solution.py:257
  21.1 107.4 %collective-permute-start.2 = (bf16[3,896,256]{2,1,0:T(8,128)(2,1)}, bf16[3,896,256]{2,1,0:T(8,128)(2,1)}, u32[]{:S(2)}, u32[]{:S(2)}) collective-permute-start(bf16[3,896,256]{2,1,0:T(8,128)(2,1)} %get-tuple-element.55), channel_id=1, source_target_pairs={{0,24},{2,26},{4,28},{6,30},{8,0},{10,2},{12,4},{14,6},{16,8},{18,... | collective-permute-start | bytes 4128776 | tf_op jit(solution)/shard_map/ppermute | solution.py:32
  24.8 123.9 %collective-permute-start.1 = (bf16[3,896,256]{2,1,0:T(8,128)(2,1)}, bf16[3,896,256]{2,1,0:T(8,128)(2,1)}, u32[]{:S(2)}, u32[]{:S(2)}) collective-permute-start(bf16[3,896,256]{2,1,0:T(8,128)(2,1)} %get-tuple-element.56), channel_id=1, source_target_pairs={{0,16},{2,18},{4,20},{6,22},{8,24},{10,26},{12,28},{14,30},{16,0},... | collective-permute-start | bytes 4128776 | tf_op jit(solution)/shard_map/ppermute | solution.py:32
  53.7 1.4 copy-start.18
  57.6 96.5 %all-to-all-start.1 = ((bf16[16,128,128]{2,1,0:T(8,128)(2,1)}), bf16[16,128,128]{2,1,0:T(8,128)(2,1)S(1)}, u32[]{:S(2)}, u32[]{:S(2)}) async-start(bf16[16,128,128]{2,1,0:T(8,128)(2,1)} %shard_map.104), calls=%async_computation.1 | async-start | bytes 1048576 | tf_op jit(solution)/shard_map/all_to_all | solution.py:266
  125.0 32.7 %copy-start.2 = (bf16[2,3,896,256]{3,2,1,0:T(8,128)(2,1)}, bf16[2,3,896,256]{3,2,1,0:T(8,128)(2,1)S(1)}, u32[]{:S(2)}) copy-start(bf16[2,3,896,256]{3,2,1,0:T(8,128)(2,1)S(1)} %pad_maximum_fusion.3.args_1_) | copy-start | bytes 8257540
  125.1 66.3 %collective-permute-start.4 = (bf16[2,3,896,256]{3,2,1,0:T(8,128)(2,1)S(1)}, bf16[2,3,896,256]{3,2,1,0:T(8,128)(2,1)}, u32[]{:S(2)}, u32[]{:S(2)}) collective-permute-start(bf16[2,3,896,256]{3,2,1,0:T(8,128)(2,1)S(1)} %pad_maximum_fusion.3.args_1_), channel_id=1, source_target_pairs={{0,4},{2,6},{4,0},{6,2},{8,12},{10,14},{12,8},{14,10},{16,20},{18,... | collective-permute-start | bytes 8257544 | tf_op jit(solution)/shard_map/ppermute | solution.py:37
  127.0 65.7 %collective-permute-start.3 = (bf16[2,3,896,256]{3,2,1,0:T(8,128)(2,1)S(1)}, bf16[2,3,896,256]{3,2,1,0:T(8,128)(2,1)}, u32[]{:S(2)}, u32[]{:S(2)}) collective-permute-start(bf16[2,3,896,256]{3,2,1,0:T(8,128)(2,1)S(1)} %pad_maximum_fusion.3.args_1_), channel_id=1, source_target_pairs={{0,2},{2,0},{4,6},{6,4},{8,10},{10,8},{12,14},{14,12},{16,18},{18,... | collective-permute-start | bytes 8257544 | tf_op jit(solution)/shard_map/ppermute | solution.py:37
  154.1 5.1 %copy-start.22 = (f32[256,32]{0,1:T(8,128)S(1)}, f32[256,32]{0,1:T(8,128)}, u32[]{:S(2)}) copy-start(f32[256,32]{0,1:T(8,128)} %get-tuple-element.70) | copy-start | bytes 98308
  154.1 5.1 %copy-start.24 = (f32[32,256]{1,0:T(8,128)S(1)}, f32[32,256]{1,0:T(8,128)}, u32[]{:S(2)}) copy-start(f32[32,256]{1,0:T(8,128)} %get-tuple-element.64) | copy-start | bytes 98308
  157.7 92.7 %collective-permute-start.10 = (bf16[2,3,896,256]{3,2,1,0:T(8,128)(2,1)}, bf16[2,3,896,256]{3,2,1,0:T(8,128)(2,1)}, u32[]{:S(2)}, u32[]{:S(2)}) collective-permute-start(bf16[2,3,896,256]{3,2,1,0:T(8,128)(2,1)} %pad_maximum_fusion.4.args_6_), channel_id=1, source_target_pairs={{0,4},{2,6},{4,0},{6,2},{8,12},{10,14},{12,8},{14,10},{16,20},{18,... | collective-permute-start | bytes 8257544 | tf_op jit(solution)/shard_map/ppermute | solution.py:37
  162.6 1.2 copy-start.17
  162.6 1.2 copy-start.21
  162.6 1.2 copy-start.25
  162.6 89.1 %collective-permute-start.9 = (bf16[2,3,896,256]{3,2,1,0:T(8,128)(2,1)}, bf16[2,3,896,256]{3,2,1,0:T(8,128)(2,1)}, u32[]{:S(2)}, u32[]{:S(2)}) collective-permute-start(bf16[2,3,896,256]{3,2,1,0:T(8,128)(2,1)} %pad_maximum_fusion.4.args_6_), channel_id=1, source_target_pairs={{0,2},{2,0},{4,6},{6,4},{8,10},{10,8},{12,14},{14,12},{16,18},{18,... | collective-permute-start | bytes 8257544 | tf_op jit(solution)/shard_map/ppermute | solution.py:37
  165.7 4.7 %dynamic-slice-start = ((f32[4096]{0:T(1024)}, s32[]{:T(128)}), f32[2048]{0:T(1024)S(1)}, s32[]{:S(2)}) async-start(f32[4096]{0:T(1024)} %param.14, s32[]{:T(128)} %select_n.81), calls=%async_computation.2 | async-start | bytes 16896 | tf_op jit(solution)/shard_map/dynamic_slice | solution.py:290
  195.6 83.2 %collective-permute-start.12 = (bf16[1,3,896,256]{3,2,1,0:T(8,128)(2,1)S(1)}, bf16[1,3,896,256]{3,2,1,0:T(8,128)(2,1)}, u32[]{:S(2)}, u32[]{:S(2)}) collective-permute-start(bf16[1,3,896,256]{3,2,1,0:T(8,128)(2,1)S(1)} %slice.49), channel_id=1, source_target_pairs={{0,2},{2,0},{4,6},{6,4},{8,10},{10,8},{12,14},{14,12},{16,18},{18,... | collective-permute-start | bytes 4128776 | tf_op jit(solution)/shard_map/ppermute | solution.py:37
  196.9 82.0 %collective-permute-start.11 = (bf16[1,3,896,256]{3,2,1,0:T(8,128)(2,1)S(1)}, bf16[1,3,896,256]{3,2,1,0:T(8,128)(2,1)}, u32[]{:S(2)}, u32[]{:S(2)}) collective-permute-start(bf16[1,3,896,256]{3,2,1,0:T(8,128)(2,1)S(1)} %slice.48), channel_id=1, source_target_pairs={{0,4},{2,6},{4,0},{6,2},{8,12},{10,14},{12,8},{14,10},{16,20},{18,... | collective-permute-start | bytes 4128776 | tf_op jit(solution)/shard_map/ppermute | solution.py:37
  197.6 54.1 %collective-permute-start.8 = (bf16[256,2048]{1,0:T(8,128)(2,1)}, bf16[256,2048]{1,0:T(8,128)(2,1)S(1)}, u32[]{:S(2)}, u32[]{:S(2)}) collective-permute-start(bf16[256,2048]{1,0:T(8,128)(2,1)} %fusion.9), channel_id=1, source_target_pairs={{0,16},{2,18},{4,20},{6,22},{8,24},{10,26},{12,28},{14,30},{16,0},... | collective-permute-start | bytes 3145736 | tf_op jit(solution)/shard_map/ppermute | solution.py:32
  250.4 22.1 %collective-permute-start.7 = (bf16[256,2048]{1,0:T(8,128)(2,1)}, bf16[256,2048]{1,0:T(8,128)(2,1)S(1)}, u32[]{:S(2)}, u32[]{:S(2)}) collective-permute-start(bf16[256,2048]{1,0:T(8,128)(2,1)} %fusion.9), channel_id=1, source_target_pairs={{0,8},{2,10},{4,12},{6,14},{8,16},{10,18},{12,20},{14,22},{16,24},... | collective-permute-start | bytes 3145736 | tf_op jit(solution)/shard_map/ppermute | solution.py:32
  279.0 29.8 %collective-permute-start.15 = (bf16[512,2048]{1,0:T(8,128)(2,1)S(1)}, bf16[512,2048]{1,0:T(8,128)(2,1)}, u32[]{:S(2)}, u32[]{:S(2)}) collective-permute-start(bf16[512,2048]{1,0:T(8,128)(2,1)S(1)} %constant_dynamic-update-slice_fusion.2), channel_id=1, source_target_pairs={{0,1},{1,0},{2,3},{3,2},{4,5},{5,4},{6,7},{7,6},{8,9},{9,8},{10,11... | collective-permute-start | bytes 6291464 | tf_op jit(solution)/shard_map/ppermute | solution.py:194
  279.1 26.2 %collective-permute-start.5 = (bf16[256,2048]{1,0:T(8,128)(2,1)}, bf16[256,2048]{1,0:T(8,128)(2,1)S(1)}, u32[]{:S(2)}, u32[]{:S(2)}) collective-permute-start(bf16[256,2048]{1,0:T(8,128)(2,1)} %fusion.9), channel_id=1, source_target_pairs={{0,24},{2,26},{4,28},{6,30},{8,0},{10,2},{12,4},{14,6},{16,8},{18,... | collective-permute-start | bytes 3145736 | tf_op jit(solution)/shard_map/ppermute | solution.py:32
  285.0 32.1 %collective-permute-start.14 = (bf16[1,3,896,256]{3,2,1,0:T(8,128)(2,1)S(1)}, bf16[1,3,896,256]{3,2,1,0:T(8,128)(2,1)S(1)}, u32[]{:S(2)}, u32[]{:S(2)}) collective-permute-start(bf16[1,3,896,256]{3,2,1,0:T(8,128)(2,1)S(1)} %slice.51), channel_id=1, source_target_pairs={{0,2},{2,0},{4,6},{6,4},{8,10},{10,8},{12,14},{14,12},{16,18},{18,... | collective-permute-start | bytes 4128776 | tf_op jit(solution)/shard_map/ppermute | solution.py:37
  285.6 31.8 %collective-permute-start.13 = (bf16[1,3,896,256]{3,2,1,0:T(8,128)(2,1)S(1)}, bf16[1,3,896,256]{3,2,1,0:T(8,128)(2,1)S(1)}, u32[]{:S(2)}, u32[]{:S(2)}) collective-permute-start(bf16[1,3,896,256]{3,2,1,0:T(8,128)(2,1)S(1)} %slice.50), channel_id=1, source_target_pairs={{0,4},{2,6},{4,0},{6,2},{8,12},{10,14},{12,8},{14,10},{16,20},{18,... | collective-permute-start | bytes 4128776 | tf_op jit(solution)/shard_map/ppermute | solution.py:37
  308.8 46.1 %collective-permute-start.6 = (bf16[512,2048]{1,0:T(8,128)(2,1)}, bf16[512,2048]{1,0:T(8,128)(2,1)}, u32[]{:S(2)}, u32[]{:S(2)}) collective-permute-start(bf16[512,2048]{1,0:T(8,128)(2,1)} %constant_dynamic-update-slice_fusion), channel_id=1, source_target_pairs={{0,1},{1,0},{2,3},{3,2},{4,5},{5,4},{6,7},{7,6},{8,9},{9,8},{10,11... | collective-permute-start | bytes 6291464 | tf_op jit(solution)/shard_map/ppermute | solution.py:194
  313.1 22.0 %copy-start.3 = (bf16[2,3,896,256]{3,2,1,0:T(8,128)(2,1)S(1)}, bf16[2,3,896,256]{3,2,1,0:T(8,128)(2,1)}, u32[]{:S(2)}) copy-start(bf16[2,3,896,256]{3,2,1,0:T(8,128)(2,1)} %copy-done.2) | copy-start | bytes 8257540
  317.2 1.1 copy-start.5
  318.3 1.1 copy-start.8
  335.1 1.3 copy-start.6
  336.4 1.3 copy-start.9
  337.7 1.2 copy-start.12
  354.9 5.0 %collective-permute-start.16 = (bf16[512,2048]{1,0:T(8,128)(2,1)}, bf16[512,2048]{1,0:T(8,128)(2,1)S(1)}, u32[]{:S(2)}, u32[]{:S(2)}) collective-permute-start(bf16[512,2048]{1,0:T(8,128)(2,1)} %dynamic-slice_bitcast_fusion.1), channel_id=1, source_target_pairs={{0,1},{1,0},{2,3},{3,2},{4,5},{5,4},{6,7},{7,6},{8,9},{9,8},{10,11... | collective-permute-start | bytes 6291464 | tf_op jit(solution)/shard_map/ppermute | solution.py:205
  357.4 3.7 copy-start.13
  363.4 47.9 %collective-permute-start.18 = (bf16[256,2048]{1,0:T(8,128)(2,1)}, bf16[256,2048]{1,0:T(8,128)(2,1)S(1)}, u32[]{:S(2)}, u32[]{:S(2)}) collective-permute-start(bf16[256,2048]{1,0:T(8,128)(2,1)} %get-tuple-element.62), channel_id=1, source_target_pairs={{0,16},{2,18},{4,20},{6,22},{8,24},{10,26},{12,28},{14,30},{16,0},... | collective-permute-start | bytes 3145736 | tf_op jit(solution)/shard_map/ppermute | solution.py:32
  363.4 17.3 %copy-start.4 = (bf16[2,3,896,256]{3,2,1,0:T(8,128)(2,1)S(1)}, bf16[2,3,896,256]{3,2,1,0:T(8,128)(2,1)}, u32[]{:S(2)}) copy-start(bf16[2,3,896,256]{3,2,1,0:T(8,128)(2,1)} %copy-done.2) | copy-start | bytes 8257540
  363.4 17.3 %copy-start.7 = (bf16[1,3,896,256]{3,2,1,0:T(8,128)(2,1)S(1)}, bf16[1,3,896,256]{3,2,1,0:T(8,128)(2,1)}, u32[]{:S(2)}) copy-start(bf16[1,3,896,256]{3,2,1,0:T(8,128)(2,1)} %copy-done.5) | copy-start | bytes 4128772
  363.4 17.4 %copy-start.10 = (bf16[1,3,896,256]{3,2,1,0:T(8,128)(2,1)S(1)}, bf16[1,3,896,256]{3,2,1,0:T(8,128)(2,1)}, u32[]{:S(2)}) copy-start(bf16[1,3,896,256]{3,2,1,0:T(8,128)(2,1)} %copy-done.8) | copy-start | bytes 4128772
  363.4 48.5 %collective-permute-start.17 = (bf16[256,2048]{1,0:T(8,128)(2,1)}, bf16[256,2048]{1,0:T(8,128)(2,1)S(1)}, u32[]{:S(2)}, u32[]{:S(2)}) collective-permute-start(bf16[256,2048]{1,0:T(8,128)(2,1)} %get-tuple-element.63), channel_id=1, source_target_pairs={{0,24},{2,26},{4,28},{6,30},{8,0},{10,2},{12,4},{14,6},{16,8},{18,... | collective-permute-start | bytes 3145736 | tf_op jit(solution)/shard_map/ppermute | solution.py:32
  380.8 1.2 copy-start.11
  394.8 23.1 %copy-start.14 = (bf16[2,512,2048]{2,1,0:T(8,128)(2,1)S(1)}, bf16[2,512,2048]{2,1,0:T(8,128)(2,1)}, u32[]{:S(2)}) copy-start(bf16[2,512,2048]{2,1,0:T(8,128)(2,1)} %shard_map.106) | copy-start | bytes 12582916
  413.7 4.2 collective-permute-start.19
  418.8 47.3 %copy-start.15 = (bf16[256,2048]{1,0:T(8,128)(2,1)S(1)}, bf16[256,2048]{1,0:T(8,128)(2,1)}, u32[]{:S(2)}) copy-start(bf16[256,2048]{1,0:T(8,128)(2,1)} %copy.39) | copy-start | bytes 3145732
  418.8 49.2 %copy-start.1 = (bf16[256,128]{1,0:T(8,128)(2,1)S(1)}, bf16[256,128]{1,0:T(8,128)(2,1)}, u32[]{:S(2)}) copy-start(bf16[256,128]{1,0:T(8,128)(2,1)} %param.11) | copy-start | bytes 196612
  418.9 47.2 %collective-permute-start.20 = (bf16[256,2048]{1,0:T(8,128)(2,1)S(1)}, bf16[256,2048]{1,0:T(8,128)(2,1)S(1)}, u32[]{:S(2)}, u32[]{:S(2)}) collective-permute-start(bf16[256,2048]{1,0:T(8,128)(2,1)S(1)} %slice.62), channel_id=1, source_target_pairs={{0,8},{2,10},{4,12},{6,14},{8,16},{10,18},{12,20},{14,22},{16,24},... | collective-permute-start | bytes 3145736 | tf_op jit(solution)/shard_map/ppermute | solution.py:32

commit v3 on v2

--- a/solution.py
+++ b/solution.py
@@ -8,6 +8,7 @@
 from jax.sharding import PartitionSpec as P
 
 MINOR = 4
+PIECES = 13
 BF = jnp.bfloat16
 F32 = jnp.float32
 
@@ -41,15 +42,29 @@
     return lax.dot_general(x, w, (((1,), (1,)), ((), ())), preferred_element_type=F32)
 
 
-def piece_ref(refs, k, m):
-    group, at = refs[5 * (k // 2) : 5 * (k // 2) + 5], k % 2
+def near_steps(major):
+    return [k for k in range(1, major) if k != major // 2]
+
+
+def piece_ref(refs, major, k, m, q):
+    own0, x0, y0, d0, e0, near, near_x, near_y, by_1, by_2, far, d_far, e_far = refs
+    half = (major - 2) // 2
+    if k == 0:
+        return (own0, x0, y0)[m].at[q] if m < 3 else (d0.at[q] if q < 2 else e0.at[0])
+    if k == major // 2:
+        if m == 0:
+            return far.at[q]
+        if m < 3:
+            return (by_1, by_2)[m - 1].at[3 * half + q]
+        return d_far.at[q] if q < 2 else e_far.at[0]
+    i = near_steps(major).index(k)
     if m < 3:
-        return group[m].at[at]
-    return group[3 + at].at[0]
+        return (near, near_x, near_y)[m].at[3 * i + q]
+    return by_2.at[3 * i + q] if i < half else by_1.at[3 * (i - half) + q]
 
 
 def gate_up_kernel(major, depth, *args):
-    count = 5 * major // 2
+    count = PIECES
     x_ref, w_refs = args[0], args[1 : 1 + count]
     h_ref, wbuf, acc, sem = args[1 + count :]
     _, rows, width = x_ref.shape
@@ -60,9 +75,10 @@
     def fetch(k):
         return [
             pltpu.make_async_copy(
-                piece_ref(w_refs, k, m).at[pl.ds(0, 2)], wbuf.at[k % 2, m], sem.at[k % 2, m]
+                piece_ref(w_refs, major, k, m, q), wbuf.at[k % 2, m, q], sem.at[k % 2, m, q]
             )
             for m in range(MINOR)
+            for q in range(2)
         ]
 
     for c in fetch(0):
@@ -96,7 +112,7 @@
 
 
 def down_kernel(major, depth, *args):
-    count = 5 * major // 2
+    count = PIECES
     h_ref, w_refs = args[0], args[1 : 1 + count]
     o_ref, wbuf, obuf, sem, osem = args[1 + count :]
     rows = h_ref.shape[0]
@@ -108,7 +124,7 @@
 
     def fetch(j):
         k, m = steps[j]
-        return pltpu.make_async_copy(piece_ref(w_refs, k, m).at[2], wbuf.at[j % 2], sem.at[j % 2])
+        return pltpu.make_async_copy(piece_ref(w_refs, major, k, m, 2), wbuf.at[j % 2], sem.at[j % 2])
 
     def put(j):
         k, m = steps[j]
@@ -154,7 +170,7 @@
 def feed_forward(normed, pieces, major, depth):
     shares, rows, share = normed.shape
     width = shares * share
-    units = pieces[0].shape[2]
+    units = pieces[0].shape[1]
     hidden = pl.pallas_call(
         functools.partial(gate_up_kernel, major, depth),
         out_shape=jax.ShapeDtypeStruct((rows, units), BF),
@@ -163,7 +179,7 @@
         scratch_shapes=[
             pltpu.VMEM((2, MINOR, 2, units, depth), BF),
             pltpu.VMEM((2, rows, units), F32),
-            pltpu.SemaphoreType.DMA((2, MINOR)),
+            pltpu.SemaphoreType.DMA((2, MINOR, 2)),
         ],
         compiler_params=pltpu.CompilerParams(vmem_limit_bytes=56 << 20),
         cost_estimate=pl.CostEstimate(
@@ -206,6 +222,12 @@
     return (keep.astype(F32) + come.astype(F32)).astype(BF)
 
 
+def return_tokens(partial, steps, major, n):
+    own = own_features(partial)
+    own = own.reshape(len(steps), own.shape[0] // len(steps), own.shape[1])
+    return [along_major(own[i], major - k, n) if k else own[i] for i, k in enumerate(steps)]
+
+
 def on_device(
     ssm_inputs,
     write_proj,
@@ -234,7 +256,12 @@
     def chunk(k):
         return lax.dynamic_index_in_dim(stacked, (a + k) % major, axis=1, keepdims=False)
 
-    got = [chunk(0)] + [along_major(chunk(k), k, n) for k in range(1, major)]
+    far = major // 2
+    near = near_steps(major)
+    half = 3 * len(near) // 2
+    got = [along_major(chunk(k), k, n) for k in near]
+    own = chunk(0)
+    pieces = [own, along_minor(own, 1, n), along_minor(own, 2, n)]
 
     x = ssm_inputs.astype(F32).reshape(toks, heads, hdim)
     scaled = x * jnp.sqrt(-jnp.expm1(2.0 * log_decay))[:, :, None]
@@ -262,16 +289,14 @@
         in_specs=[INV, INV],
         out_specs=INV,
     )(finals, decays[:, :, None])
-    before, got[1] = lax.optimization_barrier((before, got[1]))
+    before, pieces = lax.optimization_barrier((before, pieces))
     incoming = lax.all_to_all(before, "seq", 0, 0, tiled=True).reshape(feats, states)
-    incoming, *got[2:] = lax.optimization_barrier((incoming, *got[2:]))
-
-    def first_hops(g):
-        own = jnp.stack(got[g : g + 2])
-        return [own, along_minor(own, 1, n), along_minor(own, 2, n)]
-
-    def second_hops(hops):
-        return [along_minor(hops[1][:1], 2, n), along_minor(hops[2][1:], 1, n)]
+    pieces += [along_minor(pieces[1][:2], 2, n), along_minor(pieces[2][2:], 1, n)]
+    far_chunk = chunk(far)
+    incoming, far_chunk, got, pieces = lax.optimization_barrier((incoming, far_chunk, got, pieces))
+    far_own = along_major(far_chunk, far, n)
+    group = jnp.concatenate(got)
+    pieces += [group, along_minor(group, 1, n), along_minor(group, 2, n)]
 
     scores = nt(read_proj, write_proj)
     r = running.T
@@ -290,25 +315,27 @@
     gain = lax.dynamic_slice_in_dim(norm_gain, lax.axis_index("tp") * feats, feats)
     normed = (rows_f * lax.rsqrt(square_sum / (feats * tp) + 1e-05) * gain[None, :]).astype(BF)
 
-    groups = [first_hops(g) for g in range(0, major, 2)]
-    normed, groups[0] = lax.optimization_barrier((normed, groups[0]))
+    normed, far_own, pieces = lax.optimization_barrier((normed, far_own, pieces))
     tokens = [normed] + [along_major(normed, k, n) for k in range(1, major)]
+    by_1 = along_minor(jnp.concatenate([pieces[7][half:], far_own]), 1, n)
+    by_2 = along_minor(jnp.concatenate([pieces[6][:half], far_own]), 2, n)
     cut = major // 2 + 1
-    pieces = groups[0] + second_hops(groups[0])
-    tokens[1:cut], groups[1:], pieces = lax.optimization_barrier(
-        (tokens[1:cut], groups[1:], pieces)
-    )
-    pieces = pieces + sum([g + second_hops(g) for g in groups[1:]], [])
+    tokens[1:cut], by_1, by_2 = lax.optimization_barrier((tokens[1:cut], by_1, by_2))
+    last = [along_minor(by_1[half : half + 2], 2, n), along_minor(by_2[half + 2 :], 1, n)]
+    pieces += [by_1, by_2, far_own] + last
 
     order = list(range(1, major)) + [0]
-    backs = []
-    for half in (order[: major // 2], order[major // 2 :]):
-        some = jnp.concatenate([tokens[k] for k in half], axis=0)
-        partial = feed_forward(share_features(some), pieces, major, depth)
-        if backs:
-            partial, backs = lax.optimization_barrier((partial, backs))
-        own = own_features(partial).reshape(len(half), toks, feats)
-        backs += [along_major(own[i], major - k, n) if k else own[i] for i, k in enumerate(half)]
+    backs, partial = [], None
+    for half in (order[:far], order[far:]):
+        some = [tokens[k] for k in half]
+        if partial is not None:
+            some, partial = lax.optimization_barrier((some, partial))
+            backs = return_tokens(partial, order[:far], major, n)
+        after = feed_forward(share_features(jnp.concatenate(some)), pieces, major, depth)
+        if partial is not None:
+            after, backs = lax.optimization_barrier((after, backs))
+        partial = after
+    backs = backs + return_tokens(partial, order[far:], major, n)
     mlp = sum(back.astype(F32) for back in backs)
     mixed = (rows_f + mlp).astype(BF)
     return (ssd_out, mixed)

time: 469 us -> 433 us (0.923)
  starting transfers between devices: 117 us -> 80 us
    ppermute x9, waiting for transfers between devices: 101 us -> 165 us  [along_major(): return lax.ppermute(x, 'seq', route)]
    ppermute x8 -> x10, waiting for transfers between devices: 81.7 us -> 18.9 us  [along_minor(): return lax.ppermute(x, 'seq', route)]
    all_to_all x1, starting transfers between devices: 65.5 us -> 26.3 us  [on_device(): lax.all_to_all(before, 'seq', 0, 0, tiled=True).reshape(feats, states)]
    all_to_all x1, waiting for transfers between devices: 28.8 us -> 20.3 us  [on_device(): finals = lax.all_to_all(payload, 'seq', 0, 0, tiled=True)]
    another operation x5 -> x3, other arithmetic: 6.93 us -> 1.31 us  [the longest x2 5.61 us: first_hops(): own = jnp.stack(got[g:g + 2])]
    ppermute x8 -> x10, starting transfers between devices: 9.08 us -> 14 us  [along_minor(): return lax.ppermute(x, 'seq', route)]
    unnamed x56 -> x71, local copies, waits for them, and re-layouts: 12.4 us -> 13.3 us
  transfers between devices with their start and end apart: 23 -> 25, of which waited for: 16 -> 13; matrix products, arithmetic and copies ran while one was open for 10% -> 8% of each run, Pallas kernels for 13% -> 14%
where the time goes in v3:
time: 433 us; the launch traced here: 432 us
  waiting for transfers between devices  222 us (51%)
  starting transfers between devices  80 us (18%)
  Pallas kernels  60.6 us (14%)
  local copies, waits for them, and re-layouts  31.5 us (7%)
  other arithmetic  28.7 us (7%)
  matrix products  5.47 us (1%)
    ppermute x9, waiting for transfers between devices, along_major(): return lax.ppermute(x, 'seq', route)  165 us
    ppermute x9, starting transfers between devices, along_major(): return lax.ppermute(x, 'seq', route)  34.3 us
    pallas_call x2, Pallas kernels, feed_forward(): pl.pallas_call(functools.partial(gate_up_kernel, major, depth), out_shape...  32.5 us
    all_to_all x1, starting transfers between devices, on_device(): lax.all_to_all(before, 'seq', 0, 0, tiled=True).reshape(feats, states)  26.3 us
    pallas_call x2, Pallas kernels, feed_forward(): pl.pallas_call(functools.partial(down_kernel, major, depth), out_shape=ja...  25.5 us
    all_to_all x1, waiting for transfers between devices, on_device(): finals = lax.all_to_all(payload, 'seq', 0, 0, tiled=True)  20.3 us
    ppermute x10, waiting for transfers between devices, along_minor(): return lax.ppermute(x, 'seq', route)  18.9 us
    ppermute x10, starting transfers between devices, along_minor(): return lax.ppermute(x, 'seq', route)  14 us
  transfers between devices with their start and end apart: 25, of which 13 were waited for; matrix products, arithmetic and copies ran while one was open for 8% of the time, Pallas kernels for 14%

profile of v3, /device:TPU:0, one launch (start us, length us, event | category | flops | bytes accessed | tf_op | source)
XLA Modules:
  0.0 431.7 jit_solution(8778843262471097003)
XLA Ops:
  0.7 3.4 pad_maximum_fusion
  4.2 2.1 dynamic-slice_bitcast_fusion.2
  6.3 3.0 collective-permute-start.1
  9.2 1.5 collective-permute-start
  12.8 2.3 copy.33
  15.2 1.5 fusion.11
  17.1 1.0 maximum_maximum_fusion
  18.1 5.0 %all-to-all-start = ((bf16[16,144,128]{2,1,0:T(8,128)(2,1)}), bf16[16,144,128]{2,1,0:T(8,128)(2,1)S(1)}, u32[]{:S(2)}, u32[]{:S(2)}) async-start(bf16[16,144,128]{2,1,0:T(8,128)(2,1)} %maximum_maximum_fusion), calls=%async_computation | async-start | bytes 1179648 | tf_op jit(solution)/shard_map/all_to_all | solution.py:284
  23.1 3.7 collective-permute-start.3
  26.8 20.3 %all-to-all-done.finals_ref = bf16[16,144,128]{2,1,0:T(8,128)(2,1)S(1)} async-done(((bf16[16,144,128]{2,1,0:T(8,128)(2,1)}), bf16[16,144,128]{2,1,0:T(8,128)(2,1)S(1)}, u32[]{:S(2)}, u32[]{:S(2)}) %all-to-all-start) | async-done | bytes 589856 | tf_op jit(solution)/shard_map/all_to_all | solution.py:284
  47.2 1.3 copy.34.decay_ref
  48.6 2.5 shard_map.104
  51.1 26.3 %all-to-all-start.1 = ((bf16[16,128,128]{2,1,0:T(8,128)(2,1)}), bf16[16,128,128]{2,1,0:T(8,128)(2,1)}, u32[]{:S(2)}, u32[]{:S(2)}) async-start(bf16[16,128,128]{2,1,0:T(8,128)(2,1)} %shard_map.104), calls=%async_computation.1 | async-start | bytes 1048576 | tf_op jit(solution)/shard_map/all_to_all | solution.py:293
  77.5 1.9 collective-permute-start.4
  79.4 1.0 slice.55
  80.5 1.5 collective-permute-start.5
  82.0 15.3 %collective-permute-done.2 = bf16[3,896,256]{2,1,0:T(8,128)(2,1)} collective-permute-done((bf16[3,896,256]{2,1,0:T(8,128)(2,1)}, bf16[3,896,256]{2,1,0:T(8,128)(2,1)}, u32[]{:S(2)}, u32[]{:S(2)}) %collective-permute-start.2) | collective-permute-done | bytes 1376288 | tf_op jit(solution)/shard_map/ppermute | solution.py:33
  97.3 2.8 collective-permute-done.4.args_4_
  100.1 9.3 %all-to-all-done.1 = bf16[16,128,128]{2,1,0:T(8,128)(2,1)} async-done(((bf16[16,128,128]{2,1,0:T(8,128)(2,1)}), bf16[16,128,128]{2,1,0:T(8,128)(2,1)}, u32[]{:S(2)}, u32[]{:S(2)}) %all-to-all-start.1) | async-done | bytes 524320 | tf_op jit(solution)/shard_map/all_to_all | solution.py:293
  109.4 1.4 constant_dynamic-update-slice_fusion.1
  110.9 1.4 constant_dynamic-update-slice_fusion.args_6_
  114.1 3.4 fusion
  118.4 1.5 fusion.25
  119.9 1.8 multiply_reduce_fusion
  121.8 2.3 copy.39
  124.0 2.4 psum.7
  126.5 1.5 fusion.9
  128.0 49.8 %collective-permute-done.6.args_11_ = bf16[3,896,256]{2,1,0:T(8,128)(2,1)} collective-permute-done((bf16[3,896,256]{2,1,0:T(8,128)(2,1)}, bf16[3,896,256]{2,1,0:T(8,128)(2,1)}, u32[]{:S(2)}, u32[]{:S(2)}) %collective-permute-start.6) | collective-permute-done | bytes 1376288 | tf_op jit(solution)/shard_map/ppermute | solution.py:33
  177.9 1.4 slice.56
  179.3 1.4 slice.57
  180.8 1.6 pad_maximum_fusion.3
  182.3 1.4 collective-permute-start.13
  184.6 3.3 collective-permute-start.10
  187.9 65.6 %collective-permute-done.11 = bf16[256,2048]{1,0:T(8,128)(2,1)S(1)} collective-permute-done((bf16[256,2048]{1,0:T(8,128)(2,1)S(1)}, bf16[256,2048]{1,0:T(8,128)(2,1)S(1)}, u32[]{:S(2)}, u32[]{:S(2)}) %collective-permute-start.11) | collective-permute-done | bytes 1048608 | tf_op jit(solution)/shard_map/ppermute | solution.py:33
  253.5 1.2 constant_dynamic-update-slice_fusion.3
  254.7 1.0 constant_dynamic-update-slice_fusion.2
  255.7 1.0 slice.59
  256.8 1.8 collective-permute-start.16
  259.1 1.1 collective-permute-done.14
  260.2 2.5 select_bitcast_fusion.3
  262.7 2.3 pad_maximum_fusion.1.args_0_
  265.1 4.8 %collective-permute-done.16.args_13_ = bf16[1,896,256]{2,1,0:T(8,128)(2,1)} collective-permute-done((bf16[1,896,256]{2,1,0:T(8,128)(2,1)S(1)}, bf16[1,896,256]{2,1,0:T(8,128)(2,1)}, u32[]{:S(2)}, u32[]{:S(2)}) %collective-permute-start.16) | collective-permute-done | bytes 458784 | tf_op jit(solution)/shard_map/ppermute | solution.py:38
  269.9 11.3 %collective-permute-done.15.args_12_ = bf16[2,896,256]{2,1,0:T(8,128)(2,1)S(1)} collective-permute-done((bf16[2,896,256]{2,1,0:T(8,128)(2,1)S(1)}, bf16[2,896,256]{2,1,0:T(8,128)(2,1)S(1)}, u32[]{:S(2)}, u32[]{:S(2)}) %collective-permute-start.15) | collective-permute-done | bytes 917536 | tf_op jit(solution)/shard_map/ppermute | solution.py:38
  282.1 15.8 %shard_map.105.args_0_ = bf16[512,896]{1,0:T(8,128)(2,1)} custom-call(bf16[2,512,2048]{2,1,0:T(8,128)(2,1)} %pad_maximum_fusion.1.args_0_, bf16[3,896,256]{2,1,0:T(8,128)(2,1)} %copy-done.5, bf16[3,896,256]{2,1,0:T(8,128)(2,1)} %copy-done.8, bf16[3,896,256]{2,1,0:T(8,128)(2,1)} %collective-permute-done.1.args_3_, bf16[2,896,256]{2,1,0:T(8,128)(2,1)} %copy-done.11, ...), custom_call_target="tpu_custom_call" | custom-call | flops 7516192768 | bytes 14680064 | tf_op jit(solution)/shard_map/pallas_call | solution.py:174
  298.0 1.2 copy-done.15
  299.1 1.2 copy-done.21
  300.3 12.8 %shard_map.106 = bf16[2,512,2048]{2,1,0:T(8,128)(2,1)} custom-call(bf16[512,896]{1,0:T(8,128)(2,1)S(1)} %copy-done.21, bf16[3,896,256]{2,1,0:T(8,128)(2,1)S(1)} %copy-done.6, bf16[3,896,256]{2,1,0:T(8,128)(2,1)S(1)} %copy-done.9, bf16[3,896,256]{2,1,0:T(8,128)(2,1)} %collective-permute-done.1.args_3_, bf16[2,896,256]{2,1,0:T(8,128)(2,1)S(1)} %copy-done.12, ...), custom_call_target="tpu_custom_call" | custom-call | flops 3758096384 | bytes 14680064 | tf_op jit(solution)/shard_map/pallas_call | solution.py:189
  313.1 3.2 dynamic-slice_bitcast_fusion.1
  316.3 1.4 constant_dynamic-update-slice_fusion.5
  318.3 2.5 collective-permute-done.18
  320.8 3.0 fusion.2
  323.8 1.5 fusion.21
  325.6 3.8 collective-permute-start.19
  329.4 1.9 select_bitcast_fusion.1
  331.2 2.3 pad_maximum_fusion.2.args_0_
  333.6 16.7 %shard_map.107.args_0_ = bf16[512,896]{1,0:T(8,128)(2,1)} custom-call(bf16[2,512,2048]{2,1,0:T(8,128)(2,1)} %pad_maximum_fusion.2.args_0_, bf16[3,896,256]{2,1,0:T(8,128)(2,1)} %copy-done.5, bf16[3,896,256]{2,1,0:T(8,128)(2,1)} %copy-done.8, bf16[3,896,256]{2,1,0:T(8,128)(2,1)} %collective-permute-done.1.args_3_, bf16[2,896,256]{2,1,0:T(8,128)(2,1)} %copy-done.11, ...), custom_call_target="tpu_custom_call" | custom-call | flops 7516192768 | bytes 14680064 | tf_op jit(solution)/shard_map/pallas_call | solution.py:174
  350.4 1.2 copy-done.20
  351.6 12.8 %shard_map.108 = bf16[2,512,2048]{2,1,0:T(8,128)(2,1)} custom-call(bf16[512,896]{1,0:T(8,128)(2,1)S(1)} %copy-done.20, bf16[3,896,256]{2,1,0:T(8,128)(2,1)S(1)} %copy-done.7, bf16[3,896,256]{2,1,0:T(8,128)(2,1)S(1)} %copy-done.10, bf16[3,896,256]{2,1,0:T(8,128)(2,1)} %collective-permute-done.1.args_3_, bf16[2,896,256]{2,1,0:T(8,128)(2,1)S(1)} %copy-done.13, ...), custom_call_target="tpu_custom_call" | custom-call | flops 3758096384 | bytes 14680064 | tf_op jit(solution)/shard_map/pallas_call | solution.py:189
  364.3 10.6 %collective-permute-done.20 = bf16[256,2048]{1,0:T(8,128)(2,1)} collective-permute-done((bf16[256,2048]{1,0:T(8,128)(2,1)}, bf16[256,2048]{1,0:T(8,128)(2,1)}, u32[]{:S(2)}, u32[]{:S(2)}) %collective-permute-start.20) | collective-permute-done | bytes 1048608 | tf_op jit(solution)/shard_map/ppermute | solution.py:33
  375.0 1.7 dynamic-slice_bitcast_fusion
  376.8 4.1 collective-permute-done.21
  382.0 22.3 %collective-permute-start.22 = (bf16[256,2048]{1,0:T(8,128)(2,1)S(1)}, bf16[256,2048]{1,0:T(8,128)(2,1)S(1)}, u32[]{:S(2)}, u32[]{:S(2)}) collective-permute-start(bf16[256,2048]{1,0:T(8,128)(2,1)S(1)} %slice.70), channel_id=1, source_target_pairs={{0,8},{2,10},{4,12},{6,14},{8,16},{10,18},{12,20},{14,22},{16,24},... | collective-permute-start | bytes 3145736 | tf_op jit(solution)/shard_map/ppermute | solution.py:33
  404.3 24.0 %collective-permute-done.22 = bf16[256,2048]{1,0:T(8,128)(2,1)S(1)} collective-permute-done((bf16[256,2048]{1,0:T(8,128)(2,1)S(1)}, bf16[256,2048]{1,0:T(8,128)(2,1)S(1)}, u32[]{:S(2)}, u32[]{:S(2)}) %collective-permute-start.22) | collective-permute-done | bytes 1048608 | tf_op jit(solution)/shard_map/ppermute | solution.py:33
  428.3 3.4 fusion.10
  (114 shorter events, 9.7 us)
Async XLA Ops:
  0.6 113.2 %copy-start = (bf16[256,128]{1,0:T(8,128)(2,1)S(1)}, bf16[256,128]{1,0:T(8,128)(2,1)}, u32[]{:S(2)}) copy-start(bf16[256,128]{1,0:T(8,128)(2,1)} %param.11) | copy-start | bytes 196612
  4.2 6.5 %copy-start.30 = (f32[256,32]{0,1:T(8,128)S(1)}, f32[256,32]{0,1:T(8,128)}, u32[]{:S(2)}) copy-start(f32[256,32]{0,1:T(8,128)} %param.12) | copy-start | bytes 98308
  6.3 10.4 %copy-start.5 = (bf16[3,896,256]{2,1,0:T(8,128)(2,1)}, bf16[3,896,256]{2,1,0:T(8,128)(2,1)S(1)}, u32[]{:S(2)}) copy-start(bf16[3,896,256]{2,1,0:T(8,128)(2,1)S(1)} %get-tuple-element.54.args_1_) | copy-start | bytes 4128772
  6.3 44.8 %collective-permute-start.1 = (bf16[3,896,256]{2,1,0:T(8,128)(2,1)S(1)}, bf16[3,896,256]{2,1,0:T(8,128)(2,1)}, u32[]{:S(2)}, u32[]{:S(2)}) collective-permute-start(bf16[3,896,256]{2,1,0:T(8,128)(2,1)S(1)} %get-tuple-element.54.args_1_), channel_id=1, source_target_pairs={{0,4},{2,6},{4,0},{6,2},{8,12},{10,14},{12,8},{14,10},{16,20},{18,... | collective-permute-start | bytes 4128776 | tf_op jit(solution)/shard_map/ppermute | solution.py:38
  9.2 41.9 %collective-permute-start = (bf16[3,896,256]{2,1,0:T(8,128)(2,1)S(1)}, bf16[3,896,256]{2,1,0:T(8,128)(2,1)S(1)}, u32[]{:S(2)}, u32[]{:S(2)}) collective-permute-start(bf16[3,896,256]{2,1,0:T(8,128)(2,1)S(1)} %get-tuple-element.54.args_1_), channel_id=1, source_target_pairs={{0,2},{2,0},{4,6},{6,4},{8,10},{10,8},{12,14},{14,12},{16,18},{18,... | collective-permute-start | bytes 4128776 | tf_op jit(solution)/shard_map/ppermute | solution.py:38
  12.8 3.9 copy-start.29
  18.1 29.1 %all-to-all-start = ((bf16[16,144,128]{2,1,0:T(8,128)(2,1)}), bf16[16,144,128]{2,1,0:T(8,128)(2,1)S(1)}, u32[]{:S(2)}, u32[]{:S(2)}) async-start(bf16[16,144,128]{2,1,0:T(8,128)(2,1)} %maximum_maximum_fusion), calls=%async_computation | async-start | bytes 1179648 | tf_op jit(solution)/shard_map/all_to_all | solution.py:284
  23.1 58.9 %collective-permute-start.3 = (bf16[3,896,256]{2,1,0:T(8,128)(2,1)}, bf16[3,896,256]{2,1,0:T(8,128)(2,1)}, u32[]{:S(2)}, u32[]{:S(2)}) collective-permute-start(bf16[3,896,256]{2,1,0:T(8,128)(2,1)} %get-tuple-element.76), channel_id=1, source_target_pairs={{0,24},{2,26},{4,28},{6,30},{8,0},{10,2},{12,4},{14,6},{16,8},{18,... | collective-permute-start | bytes 4128776 | tf_op jit(solution)/shard_map/ppermute | solution.py:33
  26.8 70.5 %collective-permute-start.2 = (bf16[3,896,256]{2,1,0:T(8,128)(2,1)}, bf16[3,896,256]{2,1,0:T(8,128)(2,1)}, u32[]{:S(2)}, u32[]{:S(2)}) collective-permute-start(bf16[3,896,256]{2,1,0:T(8,128)(2,1)} %get-tuple-element.77), channel_id=1, source_target_pairs={{0,8},{2,10},{4,12},{6,14},{8,16},{10,18},{12,20},{14,22},{16,24},... | collective-permute-start | bytes 4128776 | tf_op jit(solution)/shard_map/ppermute | solution.py:33
  47.2 1.4 copy-start.28
  51.1 58.3 %copy-start.8 = (bf16[3,896,256]{2,1,0:T(8,128)(2,1)}, bf16[3,896,256]{2,1,0:T(8,128)(2,1)S(1)}, u32[]{:S(2)}) copy-start(bf16[3,896,256]{2,1,0:T(8,128)(2,1)S(1)} %collective-permute-done.args_2_) | copy-start | bytes 4128772
  51.1 58.3 %all-to-all-start.1 = ((bf16[16,128,128]{2,1,0:T(8,128)(2,1)}), bf16[16,128,128]{2,1,0:T(8,128)(2,1)}, u32[]{:S(2)}, u32[]{:S(2)}) async-start(bf16[16,128,128]{2,1,0:T(8,128)(2,1)} %shard_map.104), calls=%async_computation.1 | async-start | bytes 1048576 | tf_op jit(solution)/shard_map/all_to_all | solution.py:293
  77.5 22.6 %collective-permute-start.4 = (bf16[2,896,256]{2,1,0:T(8,128)(2,1)S(1)}, bf16[2,896,256]{2,1,0:T(8,128)(2,1)S(1)}, u32[]{:S(2)}, u32[]{:S(2)}) collective-permute-start(bf16[2,896,256]{2,1,0:T(8,128)(2,1)S(1)} %slice.54), channel_id=1, source_target_pairs={{0,4},{2,6},{4,0},{6,2},{8,12},{10,14},{12,8},{14,10},{16,20},{18,... | collective-permute-start | bytes 2752520 | tf_op jit(solution)/shard_map/ppermute | solution.py:38
  80.5 16.8 %collective-permute-start.5 = (bf16[1,896,256]{2,1,0:T(8,128)(2,1)S(1)}, bf16[1,896,256]{2,1,0:T(8,128)(2,1)S(1)}, u32[]{:S(2)}, u32[]{:S(2)}) collective-permute-start(bf16[1,896,256]{2,1,0:T(8,128)(2,1)S(1)} %slice.55), channel_id=1, source_target_pairs={{0,2},{2,0},{4,6},{6,4},{8,10},{10,8},{12,14},{14,12},{16,18},{18,... | collective-permute-start | bytes 1376264 | tf_op jit(solution)/shard_map/ppermute | solution.py:38
  97.3 20.2 %copy-start.17 = (bf16[1,896,256]{2,1,0:T(8,128)(2,1)}, bf16[1,896,256]{2,1,0:T(8,128)(2,1)S(1)}, u32[]{:S(2)}) copy-start(bf16[1,896,256]{2,1,0:T(8,128)(2,1)S(1)} %collective-permute-done.5.args_5_) | copy-start | bytes 1376260
  100.1 9.3 %copy-start.11 = (bf16[2,896,256]{2,1,0:T(8,128)(2,1)}, bf16[2,896,256]{2,1,0:T(8,128)(2,1)S(1)}, u32[]{:S(2)}) copy-start(bf16[2,896,256]{2,1,0:T(8,128)(2,1)S(1)} %collective-permute-done.4.args_4_) | copy-start | bytes 2752516
  110.8 3.2 copy-start.31
  112.3 5.2 %copy-start.2 = (bf16[6,896,256]{2,1,0:T(8,128)(2,1)}, bf16[6,896,256]{2,1,0:T(8,128)(2,1)S(1)}, u32[]{:S(2)}) copy-start(bf16[6,896,256]{2,1,0:T(8,128)(2,1)S(1)} %constant_dynamic-update-slice_fusion.args_6_) | copy-start | bytes 8257540
  112.3 65.6 %collective-permute-start.8 = (bf16[6,896,256]{2,1,0:T(8,128)(2,1)S(1)}, bf16[6,896,256]{2,1,0:T(8,128)(2,1)}, u32[]{:S(2)}, u32[]{:S(2)}) collective-permute-start(bf16[6,896,256]{2,1,0:T(8,128)(2,1)S(1)} %constant_dynamic-update-slice_fusion.args_6_), channel_id=1, source_target_pairs={{0,4},{2,6},{4,0},{6,2},{8,12},{10,14},{12,8},{14,10},{16,20},{18,... | collective-permute-start | bytes 8257544 | tf_op jit(solution)/shard_map/ppermute | solution.py:38
  113.3 64.6 %collective-permute-start.7 = (bf16[6,896,256]{2,1,0:T(8,128)(2,1)S(1)}, bf16[6,896,256]{2,1,0:T(8,128)(2,1)}, u32[]{:S(2)}, u32[]{:S(2)}) collective-permute-start(bf16[6,896,256]{2,1,0:T(8,128)(2,1)S(1)} %constant_dynamic-update-slice_fusion.args_6_), channel_id=1, source_target_pairs={{0,2},{2,0},{4,6},{6,4},{8,10},{10,8},{12,14},{14,12},{16,18},{18,... | collective-permute-start | bytes 8257544 | tf_op jit(solution)/shard_map/ppermute | solution.py:38
  117.5 2.4 copy-start.25
  117.5 2.4 copy-start.32
  117.5 60.4 %collective-permute-start.6 = (bf16[3,896,256]{2,1,0:T(8,128)(2,1)}, bf16[3,896,256]{2,1,0:T(8,128)(2,1)}, u32[]{:S(2)}, u32[]{:S(2)}) collective-permute-start(bf16[3,896,256]{2,1,0:T(8,128)(2,1)} %get-tuple-element.40), channel_id=1, source_target_pairs={{0,16},{2,18},{4,20},{6,22},{8,24},{10,26},{12,28},{14,30},{16,0},... | collective-permute-start | bytes 4128776 | tf_op jit(solution)/shard_map/ppermute | solution.py:33
  121.8 4.7 %dynamic-slice-start = ((f32[4096]{0:T(1024)}, s32[]{:T(128)}), f32[2048]{0:T(1024)S(1)}, s32[]{:S(2)}) async-start(f32[4096]{0:T(1024)} %param.14, s32[]{:T(128)} %select_n.83), calls=%async_computation.2 | async-start | bytes 16896 | tf_op jit(solution)/shard_map/dynamic_slice | solution.py:315
  128.0 56.6 %copy-start.26 = (bf16[256,2048]{1,0:T(8,128)(2,1)}, bf16[256,2048]{1,0:T(8,128)(2,1)S(1)}, u32[]{:S(2)}) copy-start(bf16[256,2048]{1,0:T(8,128)(2,1)S(1)} %fusion.9) | copy-start | bytes 3145732
  182.3 71.2 %collective-permute-start.13 = (bf16[6,896,256]{2,1,0:T(8,128)(2,1)S(1)}, bf16[6,896,256]{2,1,0:T(8,128)(2,1)}, u32[]{:S(2)}, u32[]{:S(2)}) collective-permute-start(bf16[6,896,256]{2,1,0:T(8,128)(2,1)S(1)} %get-tuple-element.86), channel_id=1, source_target_pairs={{0,4},{2,6},{4,0},{6,2},{8,12},{10,14},{12,8},{14,10},{16,20},{18,... | collective-permute-start | bytes 8257544 | tf_op jit(solution)/shard_map/ppermute | solution.py:38
  183.7 69.8 %collective-permute-start.12 = (bf16[6,896,256]{2,1,0:T(8,128)(2,1)S(1)}, bf16[6,896,256]{2,1,0:T(8,128)(2,1)S(1)}, u32[]{:S(2)}, u32[]{:S(2)}) collective-permute-start(bf16[6,896,256]{2,1,0:T(8,128)(2,1)S(1)} %get-tuple-element.87), channel_id=1, source_target_pairs={{0,2},{2,0},{4,6},{6,4},{8,10},{10,8},{12,14},{14,12},{16,18},{18,... | collective-permute-start | bytes 8257544 | tf_op jit(solution)/shard_map/ppermute | solution.py:38
  184.6 68.9 %collective-permute-start.11 = (bf16[256,2048]{1,0:T(8,128)(2,1)S(1)}, bf16[256,2048]{1,0:T(8,128)(2,1)S(1)}, u32[]{:S(2)}, u32[]{:S(2)}) collective-permute-start(bf16[256,2048]{1,0:T(8,128)(2,1)S(1)} %fusion.9), channel_id=1, source_target_pairs={{0,16},{2,18},{4,20},{6,22},{8,24},{10,26},{12,28},{14,30},{16,0},... | collective-permute-start | bytes 3145736 | tf_op jit(solution)/shard_map/ppermute | solution.py:33
  184.6 68.9 %collective-permute-start.10 = (bf16[256,2048]{1,0:T(8,128)(2,1)S(1)}, bf16[256,2048]{1,0:T(8,128)(2,1)S(1)}, u32[]{:S(2)}, u32[]{:S(2)}) collective-permute-start(bf16[256,2048]{1,0:T(8,128)(2,1)S(1)} %fusion.9), channel_id=1, source_target_pairs={{0,8},{2,10},{4,12},{6,14},{8,16},{10,18},{12,20},{14,22},{16,24},... | collective-permute-start | bytes 3145736 | tf_op jit(solution)/shard_map/ppermute | solution.py:33
  253.5 5.1 %copy-start.23 = (bf16[6,896,256]{2,1,0:T(8,128)(2,1)}, bf16[6,896,256]{2,1,0:T(8,128)(2,1)S(1)}, u32[]{:S(2)}) copy-start(bf16[6,896,256]{2,1,0:T(8,128)(2,1)S(1)} %collective-permute-done.12.args_9_) | copy-start | bytes 8257540
  255.7 4.5 %collective-permute-start.14 = (bf16[512,2048]{1,0:T(8,128)(2,1)}, bf16[512,2048]{1,0:T(8,128)(2,1)}, u32[]{:S(2)}, u32[]{:S(2)}) collective-permute-start(bf16[512,2048]{1,0:T(8,128)(2,1)} %constant_dynamic-update-slice_fusion.2), channel_id=1, source_target_pairs={{0,1},{1,0},{2,3},{3,2},{4,5},{5,4},{6,7},{7,6},{8,9},{9,8},{10,11... | collective-permute-start | bytes 6291464 | tf_op jit(solution)/shard_map/ppermute | solution.py:210
  255.7 57.3 %collective-permute-start.9 = (bf16[256,2048]{1,0:T(8,128)(2,1)}, bf16[256,2048]{1,0:T(8,128)(2,1)}, u32[]{:S(2)}, u32[]{:S(2)}) collective-permute-start(bf16[256,2048]{1,0:T(8,128)(2,1)} %copy-done.26), channel_id=1, source_target_pairs={{0,24},{2,26},{4,28},{6,30},{8,0},{10,2},{12,4},{14,6},{16,8},{18,... | collective-permute-start | bytes 3145736 | tf_op jit(solution)/shard_map/ppermute | solution.py:33
  256.8 13.1 %collective-permute-start.16 = (bf16[1,896,256]{2,1,0:T(8,128)(2,1)S(1)}, bf16[1,896,256]{2,1,0:T(8,128)(2,1)}, u32[]{:S(2)}, u32[]{:S(2)}) collective-permute-start(bf16[1,896,256]{2,1,0:T(8,128)(2,1)S(1)} %slice.59), channel_id=1, source_target_pairs={{0,2},{2,0},{4,6},{6,4},{8,10},{10,8},{12,14},{14,12},{16,18},{18,... | collective-permute-start | bytes 1376264 | tf_op jit(solution)/shard_map/ppermute | solution.py:38
  258.7 22.5 %collective-permute-start.15 = (bf16[2,896,256]{2,1,0:T(8,128)(2,1)S(1)}, bf16[2,896,256]{2,1,0:T(8,128)(2,1)S(1)}, u32[]{:S(2)}, u32[]{:S(2)}) collective-permute-start(bf16[2,896,256]{2,1,0:T(8,128)(2,1)S(1)} %slice.58), channel_id=1, source_target_pairs={{0,4},{2,6},{4,0},{6,2},{8,12},{10,14},{12,8},{14,10},{16,20},{18,... | collective-permute-start | bytes 2752520 | tf_op jit(solution)/shard_map/ppermute | solution.py:38
  265.1 32.8 %copy-start.3 = (bf16[6,896,256]{2,1,0:T(8,128)(2,1)S(1)}, bf16[6,896,256]{2,1,0:T(8,128)(2,1)}, u32[]{:S(2)}) copy-start(bf16[6,896,256]{2,1,0:T(8,128)(2,1)} %copy-done.2) | copy-start | bytes 8257540
  265.1 32.8 %copy-start.6 = (bf16[3,896,256]{2,1,0:T(8,128)(2,1)S(1)}, bf16[3,896,256]{2,1,0:T(8,128)(2,1)}, u32[]{:S(2)}) copy-start(bf16[3,896,256]{2,1,0:T(8,128)(2,1)} %copy-done.5) | copy-start | bytes 4128772
  265.1 32.9 %copy-start.9 = (bf16[3,896,256]{2,1,0:T(8,128)(2,1)S(1)}, bf16[3,896,256]{2,1,0:T(8,128)(2,1)}, u32[]{:S(2)}) copy-start(bf16[3,896,256]{2,1,0:T(8,128)(2,1)} %copy-done.8) | copy-start | bytes 4128772
  265.1 32.9 %copy-start.12 = (bf16[2,896,256]{2,1,0:T(8,128)(2,1)S(1)}, bf16[2,896,256]{2,1,0:T(8,128)(2,1)}, u32[]{:S(2)}) copy-start(bf16[2,896,256]{2,1,0:T(8,128)(2,1)} %copy-done.11) | copy-start | bytes 2752516
  265.1 32.9 %copy-start.18 = (bf16[1,896,256]{2,1,0:T(8,128)(2,1)S(1)}, bf16[1,896,256]{2,1,0:T(8,128)(2,1)}, u32[]{:S(2)}) copy-start(bf16[1,896,256]{2,1,0:T(8,128)(2,1)} %copy-done.17) | copy-start | bytes 1376260
  281.2 0.9 copy-start.14
  297.9 1.2 copy-start.15
  299.1 1.2 copy-start.21
  316.3 1.5 copy-start.27
  316.3 4.5 %collective-permute-start.18 = (bf16[512,2048]{1,0:T(8,128)(2,1)}, bf16[512,2048]{1,0:T(8,128)(2,1)}, u32[]{:S(2)}, u32[]{:S(2)}) collective-permute-start(bf16[512,2048]{1,0:T(8,128)(2,1)} %dynamic-slice_bitcast_fusion.1), channel_id=1, source_target_pairs={{0,1},{1,0},{2,3},{3,2},{4,5},{5,4},{6,7},{7,6},{8,9},{9,8},{10,11... | collective-permute-start | bytes 6291464 | tf_op jit(solution)/shard_map/ppermute | solution.py:221
  317.9 11.4 %collective-permute-start.17 = (bf16[512,2048]{1,0:T(8,128)(2,1)S(1)}, bf16[512,2048]{1,0:T(8,128)(2,1)}, u32[]{:S(2)}, u32[]{:S(2)}) collective-permute-start(bf16[512,2048]{1,0:T(8,128)(2,1)S(1)} %constant_dynamic-update-slice_fusion.4), channel_id=1, source_target_pairs={{0,1},{1,0},{2,3},{3,2},{4,5},{5,4},{6,7},{7,6},{8,9},{9,8},{10,11... | collective-permute-start | bytes 6291464 | tf_op jit(solution)/shard_map/ppermute | solution.py:210
  325.3 49.7 %collective-permute-start.20 = (bf16[256,2048]{1,0:T(8,128)(2,1)}, bf16[256,2048]{1,0:T(8,128)(2,1)}, u32[]{:S(2)}, u32[]{:S(2)}) collective-permute-start(bf16[256,2048]{1,0:T(8,128)(2,1)} %get-tuple-element.84), channel_id=1, source_target_pairs={{0,16},{2,18},{4,20},{6,22},{8,24},{10,26},{12,28},{14,30},{16,0},... | collective-permute-start | bytes 3145736 | tf_op jit(solution)/shard_map/ppermute | solution.py:33
  325.6 49.4 %collective-permute-start.19 = (bf16[256,2048]{1,0:T(8,128)(2,1)}, bf16[256,2048]{1,0:T(8,128)(2,1)}, u32[]{:S(2)}, u32[]{:S(2)}) collective-permute-start(bf16[256,2048]{1,0:T(8,128)(2,1)} %get-tuple-element.85), channel_id=1, source_target_pairs={{0,24},{2,26},{4,28},{6,30},{8,0},{10,2},{12,4},{14,6},{16,8},{18,... | collective-permute-start | bytes 3145736 | tf_op jit(solution)/shard_map/ppermute | solution.py:33
  333.6 16.8 %copy-start.4 = (bf16[6,896,256]{2,1,0:T(8,128)(2,1)S(1)}, bf16[6,896,256]{2,1,0:T(8,128)(2,1)}, u32[]{:S(2)}) copy-start(bf16[6,896,256]{2,1,0:T(8,128)(2,1)} %copy-done.2) | copy-start | bytes 8257540
  333.6 16.8 %copy-start.7 = (bf16[3,896,256]{2,1,0:T(8,128)(2,1)S(1)}, bf16[3,896,256]{2,1,0:T(8,128)(2,1)}, u32[]{:S(2)}) copy-start(bf16[3,896,256]{2,1,0:T(8,128)(2,1)} %copy-done.5) | copy-start | bytes 4128772
  333.6 16.8 %copy-start.10 = (bf16[3,896,256]{2,1,0:T(8,128)(2,1)S(1)}, bf16[3,896,256]{2,1,0:T(8,128)(2,1)}, u32[]{:S(2)}) copy-start(bf16[3,896,256]{2,1,0:T(8,128)(2,1)} %copy-done.8) | copy-start | bytes 4128772
  333.6 16.8 %copy-start.13 = (bf16[2,896,256]{2,1,0:T(8,128)(2,1)S(1)}, bf16[2,896,256]{2,1,0:T(8,128)(2,1)}, u32[]{:S(2)}) copy-start(bf16[2,896,256]{2,1,0:T(8,128)(2,1)} %copy-done.11) | copy-start | bytes 2752516
  333.6 16.8 %copy-start.16 = (bf16[2,896,256]{2,1,0:T(8,128)(2,1)S(1)}, bf16[2,896,256]{2,1,0:T(8,128)(2,1)}, u32[]{:S(2)}) copy-start(bf16[2,896,256]{2,1,0:T(8,128)(2,1)} %copy-done.14) | copy-start | bytes 2752516
  333.6 16.8 %copy-start.19 = (bf16[1,896,256]{2,1,0:T(8,128)(2,1)S(1)}, bf16[1,896,256]{2,1,0:T(8,128)(2,1)}, u32[]{:S(2)}) copy-start(bf16[1,896,256]{2,1,0:T(8,128)(2,1)} %copy-done.17) | copy-start | bytes 1376260
  350.4 1.2 copy-start.20
  364.3 16.6 %copy-start.22 = (bf16[2,512,2048]{2,1,0:T(8,128)(2,1)S(1)}, bf16[2,512,2048]{2,1,0:T(8,128)(2,1)}, u32[]{:S(2)}) copy-start(bf16[2,512,2048]{2,1,0:T(8,128)(2,1)} %shard_map.108) | copy-start | bytes 12582916
  376.7 4.2 collective-permute-start.21
  381.9 46.4 %copy-start.24 = (bf16[256,2048]{1,0:T(8,128)(2,1)S(1)}, bf16[256,2048]{1,0:T(8,128)(2,1)}, u32[]{:S(2)}) copy-start(bf16[256,2048]{1,0:T(8,128)(2,1)} %copy.39) | copy-start | bytes 3145732
  381.9 49.8 %copy-start.1 = (bf16[256,128]{1,0:T(8,128)(2,1)S(1)}, bf16[256,128]{1,0:T(8,128)(2,1)}, u32[]{:S(2)}) copy-start(bf16[256,128]{1,0:T(8,128)(2,1)} %param.11) | copy-start | bytes 196612
  382.0 46.3 %collective-permute-start.22 = (bf16[256,2048]{1,0:T(8,128)(2,1)S(1)}, bf16[256,2048]{1,0:T(8,128)(2,1)S(1)}, u32[]{:S(2)}, u32[]{:S(2)}) collective-permute-start(bf16[256,2048]{1,0:T(8,128)(2,1)S(1)} %slice.70), channel_id=1, source_target_pairs={{0,8},{2,10},{4,12},{6,14},{8,16},{10,18},{12,20},{14,22},{16,24},... | collective-permute-start | bytes 3145736 | tf_op jit(solution)/shard_map/ppermute | solution.py:33
